TPU v7x, 32 devices: a whole 2x2x4 slice. The times are simulated.
32 devices in a mesh: blk: 8 (over z, x), slab: 4 (over y, core).
Axes of the slice: x: 2, y: 2, z: 4, core: 2. Of those that a mesh axis runs over, the one named last changes fastest.
Arguments:
- xinv: bfloat16 [8, 4096, 4096], P('blk', None, 'slab'), may hold values from -1 to 16
- ymat: bfloat16 [8, 4096, 4096], P('blk', None, 'slab'), may hold values from -1 to 16
- basis: bfloat16 [8, 4096, 1024], P('blk', 'slab'), may hold values from -0.08118988 to 0.08118988
- pair_index: int32 [8, 2, 512], P('blk'), may hold values from 0 to 1023
- orders: int32 [8], replicated, may hold values from 1 to 512, 2048 in all
- dest: int32 [8], replicated, may hold values from 0 to 7, each once
Outputs:
- factor: float32 [8, 512, 512], P('blk', 'slab')
Inputs may be any that keep to these rules, and one draw needn't show every extreme that they name: `pair_index`: entries name columns of the block's basis. Sum of all orders is 2048; the largest equals 512. `dest`: every group receives exactly one block.
All inputs are finite; a program needn't handle non-finite values.
Results may differ from a plain program's by a relative error of at most 0.0003.
Values may be sent and summed in bfloat16 or wider, within the bound.
No kernel may reach another device: no remote copies, remote signals or barrier semaphores. Data moves between devices by JAX's collectives and lax.ppermute only.
A program may use at most 64 MiB of HBM per device.

v0:
```python
import functools

import jax
import jax.numpy as jnp
from jax import lax
from jax.experimental import pallas as pl
from jax.experimental.pallas import tpu as pltpu
from jax.sharding import PartitionSpec as P


F32 = jnp.float32
BF16 = jnp.bfloat16
LANES = 128
MICRO = 8
VMEM = pl.BlockSpec(memory_space=pltpu.VMEM)
SMEM = pl.BlockSpec(memory_space=pltpu.SMEM)
TN = (((0,), (0,)), ((), ()))


def dot_f32(a, b, dims):
    dot = functools.partial(lax.dot_general, dimension_numbers=dims, preferred_element_type=F32)
    a_hi, b_hi = a.astype(BF16), b.astype(BF16)
    a_lo = (a - a_hi.astype(F32)).astype(BF16)
    b_lo = (b - b_hi.astype(F32)).astype(BF16)
    return dot(a_hi, b_hi) + (dot(a_hi, b_lo) + dot(a_lo, b_hi))


def lane_splat(x, lane):
    return jnp.broadcast_to(x[:, lane : lane + 1], (MICRO, LANES))


def row_splat(x, row):
    return jnp.broadcast_to(x[row : row + 1, :], (MICRO, x.shape[1]))


def by_tile(f, *wide):
    tiles = [f(*[x[:, t : t + LANES] for x in wide]) for t in range(0, wide[0].shape[1], LANES)]
    return tiles[0] if len(tiles) == 1 else jnp.concatenate(tiles, axis=1)


def factor_rows(a_ref, start, width):
    for m in range(0, LANES, MICRO):
        rows = a_ref[start + m : start + m + MICRO, start : start + width]
        cols = [lane_splat(rows[:, :LANES], m + k) for k in range(MICRO)]
        low = {(i, k): row_splat(cols[k], i) for k in range(MICRO) for i in range(k, MICRO)}
        inv = []
        for k in range(MICRO):
            inv.append(lax.rsqrt(low[k, k]))
            for i in range(k + 1, MICRO):
                low[i, k] = low[i, k] * inv[k]
            for j in range(k + 1, MICRO):
                for i in range(j, MICRO):
                    low[i, j] = low[i, j] - low[i, k] * low[j, k]
        wide = [row_splat(rows, i) for i in range(MICRO)]
        for k in range(MICRO):
            wide[k] = by_tile(lambda x: x * inv[k], wide[k])
            for i in range(k + 1, MICRO):
                wide[i] = by_tile(lambda x, u: x - low[i, k] * u, wide[i], wide[k])
        sub = lax.broadcasted_iota(jnp.int32, (MICRO, width), 0)
        lane = lax.broadcasted_iota(jnp.int32, (MICRO, width), 1)
        packed = wide[0]
        for k in range(1, MICRO):
            packed = jnp.where(sub == k, wide[k], packed)
        a_ref[start + m : start + m + MICRO, start : start + width] = jnp.where(lane >= sub + m, packed, 0.0)
        for later in range(m + MICRO, LANES, MICRO):
            here = pl.ds(start + later, MICRO)
            rest = a_ref[here, start : start + width]
            part = [lane_splat(rest[:, :LANES], m + k) for k in range(MICRO)]
            for k in range(MICRO):
                for j in range(k):
                    part[k] = part[k] - low[k, j] * part[j]
                part[k] = part[k] * inv[k]
            for k in range(MICRO):
                rest = by_tile(lambda x, u: x - part[k] * u, rest, wide[k])
            a_ref[here, start : start + width] = rest


def factor_all(a_ref):
    size = a_ref.shape[0]
    for start in range(0, size, LANES):
        factor_rows(a_ref, start, size - start)
        for row in range(start + LANES, size, LANES):
            left = a_ref[start : start + LANES, row : row + LANES]
            right = a_ref[start : start + LANES, row:]
            a_ref[row : row + LANES, row:] = a_ref[row : row + LANES, row:] - dot_f32(left, right, TN)


def own_rows(a_ref, out_ref, row_start):
    share, size = out_ref.shape
    base = pl.multiple_of(row_start // LANES * LANES, LANES)
    inner = row_start - base
    for q in range(0, size, LANES):
        block = a_ref[q : q + LANES, pl.ds(base, LANES)]
        block = jnp.where(q <= base, block, 0.0).T
        if share % LANES:
            keep = (
                lax.broadcasted_iota(jnp.int32, (share, LANES), 0) + inner
                == lax.broadcasted_iota(jnp.int32, (share, LANES), 1)
            ).astype(F32)
            block = lax.dot_general(
                keep, block, (((1,), (0,)), ((), ())),
                precision=lax.Precision.HIGHEST, preferred_element_type=F32,
            )
        out_ref[:, q : q + LANES] = block


def assemble(block, row, col, order):
    rows = lax.broadcasted_iota(jnp.int32, block.shape, 0) + row
    cols = lax.broadcasted_iota(jnp.int32, block.shape, 1) + col
    return jnp.where((rows < order) & (cols < order), block, 0.0) + (rows == cols).astype(F32)


def upper_blocks(size):
    count = size // LANES
    blocks = [(i, k) for k in range(count) for i in range(k + 1)]
    return blocks[: len(blocks) // 2], blocks[len(blocks) // 2 :]


def position():
    slab = lax.axis_index("slab")
    return slab // 2, slab % 2


def factor_kernel(halves, orders_ref, mine_ref, theirs_ref, out_ref, a_ref):
    _, core = position()
    order = orders_ref[lax.axis_index("blk")]
    for turn in range(2):
        @pl.when(core == turn)
        def _():
            for ref, half in ((mine_ref, halves[turn]), (theirs_ref, halves[1 - turn])):
                for t, (i, k) in enumerate(half):
                    i, k = i * LANES, k * LANES
                    a_ref[i : i + LANES, k : k + LANES] = assemble(ref[t], i, k, order)
    factor_all(a_ref)
    own_rows(a_ref, out_ref, lax.axis_index("slab") * out_ref.shape[0])


def factor_whole_kernel(s_ref, out_ref, a_ref):
    a_ref[...] = s_ref[...]
    factor_all(a_ref)
    own_rows(a_ref, out_ref, lax.axis_index("slab") * out_ref.shape[0])


def one_hot(index, rows):
    return (lax.broadcasted_iota(jnp.int32, (rows, index.shape[1]), 0) == index).astype(F32).astype(BF16)


def select_send_kernel(index_ref, v_ref, send_ref):
    chip, _ = position()
    index = jnp.where(chip == 0, index_ref[1:2], index_ref[0:1])
    send_ref[...] = jnp.dot(v_ref[...], one_hot(index, v_ref.shape[1]), preferred_element_type=F32).astype(BF16)


def select_keep_kernel(index_ref, v_ref, send_ref, keep_ref, pay_ref):
    chip, core = position()
    index = jnp.where(chip == 0, index_ref[0:1], index_ref[1:2])
    keep_ref[...] = jnp.dot(v_ref[...], one_hot(index, v_ref.shape[1]), preferred_element_type=F32).astype(BF16)

    @pl.when(core == 0)
    def _():
        pay_ref[...] = send_ref[...]

    @pl.when(core == 1)
    def _():
        pay_ref[...] = keep_ref[...]


def split_upper(total_ref, halves, core, base, mine_ref, give_ref):
    for turn in range(2):
        @pl.when(core == turn)
        def _():
            for ref, half in ((mine_ref, halves[turn]), (give_ref, halves[1 - turn])):
                for t, (i, k) in enumerate(half):
                    i, k = i * LANES, k * LANES
                    mirror = total_ref[k : k + LANES, i : i + LANES].T
                    ref[base + t] = total_ref[i : i + LANES, k : k + LANES] + mirror


def near_unit(step):
    return step // 2


def near_kernel(halves, x_ref, y_ref, keep_ref, send_ref, cross_ref, mine_ref, give_ref, main_ref, side_ref):
    step = pl.program_id(0)
    chip, core = position()
    unit = near_unit(step)
    tile = x_ref.shape[0]
    rows = pl.ds((step % 2) * tile, tile)
    is_main = (unit == 0) | ((unit == 2) & (core == 0))

    @pl.when(step == 0)
    def _():
        main_ref[...] = jnp.zeros_like(main_ref)
        side_ref[...] = jnp.zeros_like(side_ref)

    def add(z_ref, sel_ref, left_ref, scale, total_ref):
        u = jnp.dot(z_ref[...], sel_ref[...], preferred_element_type=F32)
        u = (u * scale).astype(BF16)
        total_ref[...] += lax.dot_general(left_ref[rows, :], u, TN, preferred_element_type=F32)

    for main_side, sel_ref, total_ref in ((True, keep_ref, main_ref), (False, send_ref, side_ref)):
        for here in range(2):
            z_ref = x_ref if (here == 0) == main_side else y_ref
            at = (is_main == main_side) & (chip == here)
            pl.when(at & (unit != 2))(lambda: add(z_ref, sel_ref, sel_ref, 0.5, total_ref))
            pl.when(at & (unit == 2))(lambda: add(z_ref, sel_ref, cross_ref, 1.0, total_ref))

    @pl.when(step == pl.num_programs(0) - 1)
    def _():
        half = len(halves[0])
        split_upper(side_ref, halves, core, 0, mine_ref, give_ref)
        split_upper(main_ref, halves, core, half, mine_ref, give_ref)


def near(halves, x, y, keep, send, cross):
    depth, size = keep.shape
    tile = depth // 2

    def reads(matrix):
        def index(step):
            chip, core = position()
            unit = near_unit(step)
            is_main = (unit == 0) | ((unit == 2) & (core == 0))
            mine = is_main == (chip == matrix)
            own, other = (chip * 2 + core) * 2, (chip * 2 + 1 - core) * 2
            late = jnp.where((core == 0) == (chip == matrix), other, own + 1)
            early = jnp.where(chip == matrix, own, own)
            row = jnp.where(unit == 2, other, own) + step % 2
            after = jnp.where(step >= 2, late, early)
            return jnp.where(mine, row, after), 0

        return index

    whole = lambda step: (0, 0)
    blocks = (2 * len(halves[0]), LANES, LANES)
    return pl.pallas_call(
        functools.partial(near_kernel, halves),
        out_shape=(jax.ShapeDtypeStruct(blocks, F32), jax.ShapeDtypeStruct(blocks, F32)),
        grid=(6,),
        in_specs=[
            pl.BlockSpec((tile, depth), reads(0)),
            pl.BlockSpec((tile, depth), reads(1)),
            pl.BlockSpec(keep.shape, whole),
            pl.BlockSpec(keep.shape, whole),
            pl.BlockSpec(keep.shape, whole),
        ],
        out_specs=(
            pl.BlockSpec(blocks, lambda step: (0, 0, 0)),
            pl.BlockSpec(blocks, lambda step: (0, 0, 0)),
        ),
        scratch_shapes=[pltpu.VMEM((size, size), F32), pltpu.VMEM((size, size), F32)],
        cost_estimate=pl.CostEstimate(
            flops=6 * depth * size * (depth + size), bytes_accessed=6 * depth * (depth + size), transcendentals=0
        ),
        name="near",
    )(x, y, keep, send, cross)


def far_products_kernel(x_ref, y_ref, keep_ref, give_ref, stay_ref):
    chip, _ = position()
    step = pl.program_id(0)
    for here, z_ref in ((0, x_ref), (1, y_ref)):
        for turn, out_ref in ((0, give_ref), (1, stay_ref)):
            @pl.when((chip == here) & (step // 2 == turn))
            def _():
                out_ref[...] = jnp.dot(z_ref[...], keep_ref[...], preferred_element_type=F32).astype(BF16)


def far_products(x, y, keep):
    depth, size = keep.shape
    tile = depth // 2

    def reads(matrix):
        def index(step):
            chip, core = position()
            holder = jnp.where(step < 2, 1 - core, core)
            row = ((1 - chip) * 2 + holder) * 2 + step % 2
            return jnp.where(chip == matrix, row, 0), 0

        return index

    return pl.pallas_call(
        far_products_kernel,
        out_shape=(jax.ShapeDtypeStruct(keep.shape, BF16), jax.ShapeDtypeStruct(keep.shape, BF16)),
        grid=(4,),
        in_specs=[
            pl.BlockSpec((tile, depth), reads(0)),
            pl.BlockSpec((tile, depth), reads(1)),
            pl.BlockSpec(keep.shape, lambda step: (0, 0)),
        ],
        out_specs=(
            pl.BlockSpec((tile, size), lambda step: (jnp.minimum(step, 1), 0)),
            pl.BlockSpec((tile, size), lambda step: (jnp.maximum(step - 2, 0), 0)),
        ),
        cost_estimate=pl.CostEstimate(
            flops=4 * depth * depth * size, bytes_accessed=4 * depth * (depth + size), transcendentals=0
        ),
        name="far_products",
    )(x, y, keep)


def far_kernel(halves, sel_ref, own_ref, other_ref, mine_ref, give_ref, total_ref):
    _, core = position()
    both = (own_ref[...].astype(F32) + other_ref[...].astype(F32)).astype(BF16)
    total_ref[...] = lax.dot_general(sel_ref[...], both, TN, preferred_element_type=F32)
    split_upper(total_ref, halves, core, 0, mine_ref, give_ref)


def select_columns(v, index):
    hot = (lax.broadcasted_iota(jnp.int32, (v.shape[1], index.shape[0]), 0) == index[None, :]).astype(BF16)
    return jnp.dot(v, hot, preferred_element_type=F32).astype(BF16)


def place(own, dest, groups):
    source = jnp.argmax(dest[None, :] == jnp.arange(groups, dtype=dest.dtype)[:, None], axis=1)
    pieces = own.reshape(groups, own.shape[0] // groups, own.shape[1])
    pieces = lax.all_to_all(pieces, "blk", 0, 0)
    pieces = jnp.take(pieces, source, axis=0)
    pieces = lax.all_to_all(pieces, "blk", 0, 0)
    return pieces.reshape(own.shape)


def two_chips(x, y, v, index, orders, dest):
    slabs, groups = lax.axis_size("slab"), lax.axis_size("blk")
    depth, size = v.shape[0], index.shape[1]
    halves = upper_blocks(size)
    half = len(halves[0])
    to_core = [(s, s ^ 1) for s in range(slabs)]
    to_chip = [(s, s ^ 2) for s in range(slabs)]
    picked = jax.ShapeDtypeStruct((depth, size), BF16)
    blocks = jax.ShapeDtypeStruct((half, LANES, LANES), F32)

    send = pl.pallas_call(
        select_send_kernel, out_shape=picked, in_specs=[VMEM] * 2, out_specs=VMEM, name="select_send"
    )(index, v)
    far = lax.ppermute(send, "slab", to_chip)
    keep, pay = pl.pallas_call(
        select_keep_kernel, out_shape=(picked, picked), in_specs=[VMEM] * 3, out_specs=(VMEM, VMEM),
        name="select_keep",
    )(index, v, send)
    cross = lax.ppermute(pay, "slab", to_core)
    mine, give = near(halves, x, y, keep, send, cross)
    got = lax.ppermute(give, "slab", to_core)
    far_give, far_stay = far_products(x, y, keep)
    far_got = lax.ppermute(far_give, "slab", to_core)
    side_sum = mine[:half] + got[:half]
    early = lax.ppermute(side_sum, "slab", to_chip)
    far_mine, far_give = pl.pallas_call(
        functools.partial(far_kernel, halves),
        out_shape=(blocks, blocks),
        in_specs=[VMEM] * 3,
        out_specs=(VMEM, VMEM),
        scratch_shapes=[pltpu.VMEM((size, size), F32)],
        cost_estimate=pl.CostEstimate(
            flops=2 * depth * size * size, bytes_accessed=6 * depth * size, transcendentals=0
        ),
        name="far",
    )(far, far_stay, far_got)
    total = (mine[half:] + got[half:]) + early + (far_mine + lax.ppermute(far_give, "slab", to_core))
    schur = total * lax.ppermute(total, "slab", to_chip)
    other = lax.ppermute(schur, "slab", to_core)
    own = pl.pallas_call(
        functools.partial(factor_kernel, halves),
        out_shape=jax.ShapeDtypeStruct((size // slabs, size), F32),
        in_specs=[SMEM, VMEM, VMEM],
        out_specs=VMEM,
        scratch_shapes=[pltpu.VMEM((size, size), F32)],
        name="factor",
    )(orders, schur, other)
    return place(own, dest, groups)


def any_chips(x, y, v, index, orders, dest):
    slabs, groups = lax.axis_size("slab"), lax.axis_size("blk")
    first, second = index
    order = orders[lax.axis_index("blk")]
    size = first.shape[0]
    share = size // slabs
    slab = lax.axis_index("slab")
    row_start = slab * share

    def pairing(z, index):
        picked = select_columns(v, index)
        every = lax.all_gather(picked, "slab", axis=0, tiled=True)
        c = lax.dot_general(every, z, TN, preferred_element_type=F32).astype(BF16)
        return jnp.dot(c, picked, preferred_element_type=F32)

    both = jnp.concatenate([pairing(x, first), pairing(y, second)], axis=1)
    both = lax.psum_scatter(both, "slab", scatter_dimension=0, tiled=True)
    schur = both[:, :size] * both[:, size:]
    row_ids = row_start + jnp.arange(share, dtype=jnp.int32)
    col_ids = jnp.arange(size, dtype=jnp.int32)
    mask = (row_ids[:, None] < order) & (col_ids[None, :] < order)
    schur = jnp.where(mask, schur, 0.0) + (row_ids[:, None] == col_ids[None, :]).astype(F32)
    whole = lax.all_gather(schur, "slab", axis=0, tiled=True)
    whole = 0.5 * (whole + whole.T)
    own = pl.pallas_call(
        factor_whole_kernel,
        out_shape=jax.ShapeDtypeStruct((share, size), F32),
        in_specs=[VMEM],
        out_specs=VMEM,
        scratch_shapes=[pltpu.VMEM((size, size), F32)],
        name="factor",
    )(whole)
    return place(own, dest, groups)


def on_device(xinv, ymat, basis, pair_index, orders, dest):
    body = two_chips if lax.axis_size("slab") == 4 else any_chips
    return body(xinv[0], ymat[0], basis[0], pair_index[0], orders, dest)[None]


def solution(mesh):
    return jax.shard_map(
        on_device,
        mesh=mesh,
        in_specs=(
            P("blk", None, "slab"),
            P("blk", None, "slab"),
            P("blk", "slab", None),
            P("blk", None, None),
            P(),
            P(),
        ),
        out_specs=P("blk", "slab", None),
        check_vma=False,
    )
```

profile of v0, /device:TPU:0, one launch (start us, length us, event | category | flops | bytes accessed | tf_op | source)
XLA Modules:
  0.0 112.6 jit_solution(6211772138176473989)
XLA Ops:
  0.0 3.9 %select_send.1.send_ref = bf16[1024,512]{1,0:T(8,128)(2,1)} custom-call(s32[2,512]{1,0:T(2,128)} %bitcast.14, bf16[1024,1024]{1,0:T(8,128)(2,1)} %bitcast.10), custom_call_target="tpu_custom_call" | custom-call | tf_op jit(solution)/shard_map/select_send/pallas_call | solution.py:333
  3.9 4.5 %select_keep.1 = (bf16[1024,512]{1,0:T(8,128)(2,1)}, bf16[1024,512]{1,0:T(8,128)(2,1)}) custom-call(s32[2,512]{1,0:T(2,128)} %bitcast.15, bf16[1024,1024]{1,0:T(8,128)(2,1)} %bitcast.11, bf16[1024,512]{1,0:T(8,128)(2,1)} %select_send.1.send_ref), custom_call_target="tpu_custom_call" | custom-call | tf_op jit(solution)/shard_map/select_keep/pallas_call | solution.py:337
  8.9 2.5 %collective-permute-start.3 = (bf16[1024,512]{1,0:T(8,128)(2,1)}, bf16[1024,512]{1,0:T(8,128)(2,1)S(1)}, u32[]{:S(2)}, u32[]{:S(2)}) collective-permute-start(bf16[1024,512]{1,0:T(8,128)(2,1)} %select_send.1.send_ref), channel_id=1, source_target_pairs={{0,2},{1,3},{2,0},{3,1},{4,6},{5,7},{6,4},{7,5},{8,10},{9,11},{10,... | collective-permute-start | bytes 3145736 | tf_op jit(solution)/shard_map/ppermute | solution.py:336
  11.4 6.5 %far_products.1 = (bf16[1024,512]{1,0:T(8,128)(2,1)}, bf16[1024,512]{1,0:T(8,128)(2,1)}) custom-call(bf16[4096,1024]{1,0:T(8,128)(2,1)} %bitcast.6, bf16[4096,1024]{1,0:T(8,128)(2,1)} %bitcast.8, bf16[1024,512]{1,0:T(8,128)(2,1)} %get-tuple-element.15.keep_ref), custom_call_target="tpu_custom_call" | custom-call | flops 2147483648 | bytes 6291456 | tf_op jit(solution)/shard_map/far_products/pallas_call | solution.py:282
  18.2 1.0 copy-done.3
  19.1 11.5 %near.1 = (f32[10,128,128]{2,1,0:T(8,128)}, f32[10,128,128]{2,1,0:T(8,128)}) custom-call(bf16[4096,1024]{1,0:T(8,128)(2,1)} %bitcast.7, bf16[4096,1024]{1,0:T(8,128)(2,1)} %bitcast.9, bf16[1024,512]{1,0:T(8,128)(2,1)} %get-tuple-element.15.keep_ref, bf16[1024,512]{1,0:T(8,128)(2,1)} %select_send.1.send_ref, bf16[1024,512]{1,0:T(8,128)(2,1)} %copy-done.3), custom_call_target="tpu_custom_call" | custom-call | flops 4831838208 | bytes 9437184 | tf_op jit(solution)/shard_map/near/pallas_call | solution.py:236
  31.0 4.5 %collective-permute-done.3.sel_ref = bf16[1024,512]{1,0:T(8,128)(2,1)S(1)} collective-permute-done((bf16[1024,512]{1,0:T(8,128)(2,1)}, bf16[1024,512]{1,0:T(8,128)(2,1)S(1)}, u32[]{:S(2)}, u32[]{:S(2)}) %collective-permute-start.3) | collective-permute-done | bytes 1048608 | tf_op jit(solution)/shard_map/ppermute | solution.py:336
  35.5 1.0 copy-done.1
  36.8 3.6 %far.1 = (f32[5,128,128]{2,1,0:T(8,128)}, f32[5,128,128]{2,1,0:T(8,128)}) custom-call(bf16[1024,512]{1,0:T(8,128)(2,1)} %copy-done.1, bf16[1024,512]{1,0:T(8,128)(2,1)} %get-tuple-element.19.own_ref, bf16[1024,512]{1,0:T(8,128)(2,1)} %copy-done.2), custom_call_target="tpu_custom_call" | custom-call | flops 536870912 | bytes 3145728 | tf_op jit(solution)/shard_map/far/pallas_call | solution.py:348
  40.4 1.0 slice_add_fusion
  41.4 1.8 %collective-permute-start.2 = (f32[5,128,128]{2,1,0:T(8,128)S(1)}, f32[5,128,128]{2,1,0:T(8,128)S(1)}, u32[]{:S(2)}, u32[]{:S(2)}) collective-permute-start(f32[5,128,128]{2,1,0:T(8,128)S(1)} %slice_add_fusion), channel_id=1, source_target_pairs={{0,2},{1,3},{2,0},{3,1},{4,6},{5,7},{6,4},{7,5},{8,10},{9,11},{10,... | collective-permute-start | bytes 983048 | tf_op jit(solution)/shard_map/ppermute | solution.py:347
  43.3 8.4 %collective-permute-done.2 = f32[5,128,128]{2,1,0:T(8,128)S(1)} collective-permute-done((f32[5,128,128]{2,1,0:T(8,128)S(1)}, f32[5,128,128]{2,1,0:T(8,128)S(1)}, u32[]{:S(2)}, u32[]{:S(2)}) %collective-permute-start.2) | collective-permute-done | bytes 327712 | tf_op jit(solution)/shard_map/ppermute | solution.py:347
  51.6 1.2 %fusion.1 = f32[5,128,128]{2,1,0:T(8,128)S(1)} fusion(f32[5,128,128]{2,1,0:T(8,128)S(1)} %collective-permute-done.2, f32[10,128,128]{2,1,0:T(8,128)S(1)} %collective-permute-done.1, f32[5,128,128]{2,1,0:T(8,128)} %get-tuple-element.21, f32[5,128,128]{2,1,0:T(8,128)S(1)} %collective-permute-done.5, f32[10,128,128]{2,1,0:T(8,128)} %get-tuple-element.17), kind=kLoop, calls=%fused_computation.4 | loop fusion | flops 327680 | bytes 1966080 | tf_op jit(solution)/shard_map/add | solution.py:359
  52.8 1.8 %collective-permute-start.6 = (f32[5,128,128]{2,1,0:T(8,128)S(1)}, f32[5,128,128]{2,1,0:T(8,128)S(1)}, u32[]{:S(2)}, u32[]{:S(2)}) collective-permute-start(f32[5,128,128]{2,1,0:T(8,128)S(1)} %fusion.1), channel_id=1, source_target_pairs={{0,2},{1,3},{2,0},{3,1},{4,6},{5,7},{6,4},{7,5},{8,10},{9,11},{10,... | collective-permute-start | bytes 983048 | tf_op jit(solution)/shard_map/ppermute | solution.py:360
  54.6 7.5 %collective-permute-done.6 = f32[5,128,128]{2,1,0:T(8,128)S(1)} collective-permute-done((f32[5,128,128]{2,1,0:T(8,128)S(1)}, f32[5,128,128]{2,1,0:T(8,128)S(1)}, u32[]{:S(2)}, u32[]{:S(2)}) %collective-permute-start.6) | collective-permute-done | bytes 327712 | tf_op jit(solution)/shard_map/ppermute | solution.py:360
  62.3 0.6 iota_reduce_fusion
  62.9 1.0 collective-permute-done.7.theirs_ref
  63.9 0.7 copy-done.4
  64.6 19.5 %factor.1 = f32[128,512]{1,0:T(8,128)} custom-call(s32[8]{0:T(128)} %orders_ref.1, f32[5,128,128]{2,1,0:T(8,128)} %copy-done, f32[5,128,128]{2,1,0:T(8,128)} %copy-done.4), custom_call_target="tpu_custom_call" | custom-call | tf_op jit(solution)/shard_map/factor/pallas_call | solution.py:362
  84.1 6.0 %all-to-all-start = ((f32[8,16,512]{2,1,0:T(8,128)}), f32[8,16,512]{2,1,0:T(8,128)S(1)}, u32[]{:S(2)}, u32[]{:S(2)}) async-start(f32[8,16,512]{2,1,0:T(8,128)} %bitcast.12), calls=%async_computation | async-start | bytes 524288 | tf_op jit(solution)/shard_map/all_to_all | solution.py:317
  90.1 9.2 %all-to-all-done = f32[8,16,512]{2,1,0:T(8,128)S(1)} async-done(((f32[8,16,512]{2,1,0:T(8,128)}), f32[8,16,512]{2,1,0:T(8,128)S(1)}, u32[]{:S(2)}, u32[]{:S(2)}) %all-to-all-start) | async-done | bytes 262176 | tf_op jit(solution)/shard_map/all_to_all | solution.py:317
  99.3 0.6 gather_fusion
  100.0 12.0 %all_to_all.10 = f32[8,16,512]{2,1,0:T(8,128)S(1)} all-to-all(f32[8,16,512]{2,1,0:T(8,128)S(1)} %broadcast_select_fusion), channel_id=1, replica_groups=mesh['blk'=8,'slab'=4] {'blk'}, dimensions={0} | all-to-all | bytes 524288 | tf_op jit(solution)/shard_map/all_to_all | solution.py:319
  111.9 0.7 copy.8
  (23 shorter events, 1.6 us)
Async XLA Ops:
  8.4 9.8 %collective-permute-start = (bf16[1024,512]{1,0:T(8,128)(2,1)}, bf16[1024,512]{1,0:T(8,128)(2,1)S(1)}, u32[]{:S(2)}, u32[]{:S(2)}) collective-permute-start(bf16[1024,512]{1,0:T(8,128)(2,1)} %get-tuple-element.16), channel_id=1, source_target_pairs={{0,1},{1,0},{2,3},{3,2},{4,5},{5,4},{6,7},{7,6},{8,9},{9,8},{10,11... | collective-permute-start | bytes 3145736 | tf_op jit(solution)/shard_map/ppermute | solution.py:341
  8.9 26.5 %collective-permute-start.3 = (bf16[1024,512]{1,0:T(8,128)(2,1)}, bf16[1024,512]{1,0:T(8,128)(2,1)S(1)}, u32[]{:S(2)}, u32[]{:S(2)}) collective-permute-start(bf16[1024,512]{1,0:T(8,128)(2,1)} %select_send.1.send_ref), channel_id=1, source_target_pairs={{0,2},{1,3},{2,0},{3,1},{4,6},{5,7},{6,4},{7,5},{8,10},{9,11},{10,... | collective-permute-start | bytes 3145736 | tf_op jit(solution)/shard_map/ppermute | solution.py:336
  18.0 44.3 %copy-start.5 = (s32[8]{0:T(128)S(1)}, s32[8]{0:T(128)}, u32[]{:S(2)}) copy-start(s32[8]{0:T(128)} %param.11) | copy-start | bytes 100
  18.0 17.5 %collective-permute-start.4 = (bf16[1024,512]{1,0:T(8,128)(2,1)}, bf16[1024,512]{1,0:T(8,128)(2,1)S(1)}, u32[]{:S(2)}, u32[]{:S(2)}) collective-permute-start(bf16[1024,512]{1,0:T(8,128)(2,1)} %get-tuple-element.20), channel_id=1, source_target_pairs={{0,1},{1,0},{2,3},{3,2},{4,5},{5,4},{6,7},{7,6},{8,9},{9,8},{10,11... | collective-permute-start | bytes 3145736 | tf_op jit(solution)/shard_map/ppermute | solution.py:345
  18.2 1.0 copy-start.3
  30.7 9.7 %collective-permute-start.1 = (f32[10,128,128]{2,1,0:T(8,128)}, f32[10,128,128]{2,1,0:T(8,128)S(1)}, u32[]{:S(2)}, u32[]{:S(2)}) collective-permute-start(f32[10,128,128]{2,1,0:T(8,128)} %get-tuple-element.18), channel_id=1, source_target_pairs={{0,1},{1,0},{2,3},{3,2},{4,5},{5,4},{6,7},{7,6},{8,9},{9,8},{10,11... | collective-permute-start | bytes 1966088 | tf_op jit(solution)/shard_map/ppermute | solution.py:343
  35.5 1.0 copy-start.1
  35.5 1.3 %copy-start.2 = (bf16[1024,512]{1,0:T(8,128)(2,1)}, bf16[1024,512]{1,0:T(8,128)(2,1)S(1)}, u32[]{:S(2)}) copy-start(bf16[1024,512]{1,0:T(8,128)(2,1)S(1)} %collective-permute-done.4.other_ref) | copy-start | bytes 3145732
  40.4 2.8 %collective-permute-start.5 = (f32[5,128,128]{2,1,0:T(8,128)}, f32[5,128,128]{2,1,0:T(8,128)S(1)}, u32[]{:S(2)}, u32[]{:S(2)}) collective-permute-start(f32[5,128,128]{2,1,0:T(8,128)} %get-tuple-element.22), channel_id=1, source_target_pairs={{0,1},{1,0},{2,3},{3,2},{4,5},{5,4},{6,7},{7,6},{8,9},{9,8},{10,11... | collective-permute-start | bytes 983048 | tf_op jit(solution)/shard_map/ppermute | solution.py:359
  41.4 10.2 %collective-permute-start.2 = (f32[5,128,128]{2,1,0:T(8,128)S(1)}, f32[5,128,128]{2,1,0:T(8,128)S(1)}, u32[]{:S(2)}, u32[]{:S(2)}) collective-permute-start(f32[5,128,128]{2,1,0:T(8,128)S(1)} %slice_add_fusion), channel_id=1, source_target_pairs={{0,2},{1,3},{2,0},{3,1},{4,6},{5,7},{6,4},{7,5},{8,10},{9,11},{10,... | collective-permute-start | bytes 983048 | tf_op jit(solution)/shard_map/ppermute | solution.py:347
  52.8 9.3 %collective-permute-start.6 = (f32[5,128,128]{2,1,0:T(8,128)S(1)}, f32[5,128,128]{2,1,0:T(8,128)S(1)}, u32[]{:S(2)}, u32[]{:S(2)}) collective-permute-start(f32[5,128,128]{2,1,0:T(8,128)S(1)} %fusion.1), channel_id=1, source_target_pairs={{0,2},{1,3},{2,0},{3,1},{4,6},{5,7},{6,4},{7,5},{8,10},{9,11},{10,... | collective-permute-start | bytes 983048 | tf_op jit(solution)/shard_map/ppermute | solution.py:360
  62.2 1.7 %copy-start = (f32[5,128,128]{2,1,0:T(8,128)}, f32[5,128,128]{2,1,0:T(8,128)S(1)}, u32[]{:S(2)}) copy-start(f32[5,128,128]{2,1,0:T(8,128)S(1)} %mul.3.mine_ref) | copy-start | bytes 983044
  62.2 1.7 %collective-permute-start.7 = (f32[5,128,128]{2,1,0:T(8,128)S(1)}, f32[5,128,128]{2,1,0:T(8,128)S(1)}, u32[]{:S(2)}, u32[]{:S(2)}) collective-permute-start(f32[5,128,128]{2,1,0:T(8,128)S(1)} %mul.3.mine_ref), channel_id=1, source_target_pairs={{0,1},{1,0},{2,3},{3,2},{4,5},{5,4},{6,7},{7,6},{8,9},{9,8},{10,11... | collective-permute-start | bytes 983048 | tf_op jit(solution)/shard_map/ppermute | solution.py:361
  63.9 0.7 copy-start.4
  84.1 15.2 %all-to-all-start = ((f32[8,16,512]{2,1,0:T(8,128)}), f32[8,16,512]{2,1,0:T(8,128)S(1)}, u32[]{:S(2)}, u32[]{:S(2)}) async-start(f32[8,16,512]{2,1,0:T(8,128)} %bitcast.12), calls=%async_computation | async-start | bytes 524288 | tf_op jit(solution)/shard_map/all_to_all | solution.py:317
where the time goes:
time: 113 us
  Pallas kernels  49.6 us (44%)
  waiting for transfers between devices  30.6 us (27%)
  starting transfers between devices  13.2 us (12%)
  blocking collectives  12 us (11%)
  local copies, waits for them, and re-layouts  4.27 us (4%)
  other arithmetic  2.95 us (3%)
    pallas_call x1, Pallas kernels, two_chips(): pl.pallas_call(functools.partial(factor_kernel, halves), out_shape=jax.Sh...  19.5 us
    all_to_all x1, blocking collectives, place(): pieces = lax.all_to_all(pieces, 'blk', 0, 0)  12 us
    pallas_call x1, Pallas kernels, near(): pl.pallas_call(functools.partial(near_kernel, halves), out_shape=(jax.Sha...  11.5 us
    all_to_all x1, waiting for transfers between devices, place(): pieces = lax.all_to_all(pieces, 'blk', 0, 0)  9.18 us
    ppermute x1, waiting for transfers between devices, two_chips(): early = lax.ppermute(side_sum, 'slab', to_chip)  8.38 us
    ppermute x1, waiting for transfers between devices, two_chips(): schur = total * lax.ppermute(total, 'slab', to_chip)  7.53 us
    pallas_call x1, Pallas kernels, far_products(): pl.pallas_call(far_products_kernel, out_shape=(jax.ShapeDtypeStruct(keep....  6.54 us
    all_to_all x1, starting transfers between devices, place(): pieces = lax.all_to_all(pieces, 'blk', 0, 0)  6.01 us
  transfers between devices with their start and end apart: 9, of which 5 were waited for; matrix products, arithmetic and copies ran while one was open for 1% of the time, Pallas kernels for 19%

commit v1 on v0

--- a/solution.py
+++ b/solution.py
@@ -12,6 +12,7 @@
 BF16 = jnp.bfloat16
 LANES = 128
 MICRO = 8
+GROUP = 4
 VMEM = pl.BlockSpec(memory_space=pltpu.VMEM)
 SMEM = pl.BlockSpec(memory_space=pltpu.SMEM)
 TN = (((0,), (0,)), ((), ()))
@@ -26,7 +27,7 @@
 
 
 def lane_splat(x, lane):
-    return jnp.broadcast_to(x[:, lane : lane + 1], (MICRO, LANES))
+    return jnp.take_along_axis(x, jnp.full((MICRO, LANES), lane, jnp.int32), axis=1)
 
 
 def row_splat(x, row):
@@ -39,9 +40,15 @@
 
 
 def factor_rows(a_ref, start, width):
-    for m in range(0, LANES, MICRO):
-        rows = a_ref[start + m : start + m + MICRO, start : start + width]
-        cols = [lane_splat(rows[:, :LANES], m + k) for k in range(MICRO)]
+    cols = None
+    span = slice(start, start + width)
+    count = LANES // MICRO
+    for m in range(count):
+        base = MICRO * m
+        here = slice(start + base, start + base + MICRO)
+        rows = a_ref[here, span]
+        if cols is None:
+            cols = [lane_splat(rows[:, :LANES], base + k) for k in range(MICRO)]
         low = {(i, k): row_splat(cols[k], i) for k in range(MICRO) for i in range(k, MICRO)}
         inv = []
         for k in range(MICRO):
@@ -61,18 +68,31 @@
         packed = wide[0]
         for k in range(1, MICRO):
             packed = jnp.where(sub == k, wide[k], packed)
-        a_ref[start + m : start + m + MICRO, start : start + width] = jnp.where(lane >= sub + m, packed, 0.0)
-        for later in range(m + MICRO, LANES, MICRO):
-            here = pl.ds(start + later, MICRO)
-            rest = a_ref[here, start : start + width]
-            part = [lane_splat(rest[:, :LANES], m + k) for k in range(MICRO)]
+        a_ref[here, span] = jnp.where(lane >= sub + base, packed, 0.0)
+        group_end = (m // GROUP + 1) * GROUP
+        cols = None
+        for later in range(m + 1, min(group_end + 1, count)):
+            there = slice(start + MICRO * later, start + MICRO * later + MICRO)
+            rest = a_ref[there, span]
+            head = rest[:, :LANES]
+            part = [lane_splat(head, base + k) for k in range(MICRO)]
             for k in range(MICRO):
                 for j in range(k):
                     part[k] = part[k] - low[k, j] * part[j]
                 part[k] = part[k] * inv[k]
+            if later == m + 1:
+                cols = [lane_splat(head, MICRO * later + j) for j in range(MICRO)]
+                for k in range(MICRO):
+                    for j in range(MICRO):
+                        cols[j] = cols[j] - part[k] * row_splat(part[k], j)
             for k in range(MICRO):
                 rest = by_tile(lambda x, u: x - part[k] * u, rest, wide[k])
-            a_ref[here, start : start + width] = rest
+            a_ref[there, span] = rest
+        if m + 1 == group_end and group_end + 1 < count:
+            done = a_ref[start + MICRO * (group_end - GROUP) : start + MICRO * group_end, span]
+            first = MICRO * (group_end + 1)
+            there = slice(start + first, start + LANES)
+            a_ref[there, span] = a_ref[there, span] - dot_f32(done[:, :LANES], done, TN)[first:]
 
 
 def factor_all(a_ref):
@@ -141,30 +161,6 @@
     own_rows(a_ref, out_ref, lax.axis_index("slab") * out_ref.shape[0])
 
 
-def one_hot(index, rows):
-    return (lax.broadcasted_iota(jnp.int32, (rows, index.shape[1]), 0) == index).astype(F32).astype(BF16)
-
-
-def select_send_kernel(index_ref, v_ref, send_ref):
-    chip, _ = position()
-    index = jnp.where(chip == 0, index_ref[1:2], index_ref[0:1])
-    send_ref[...] = jnp.dot(v_ref[...], one_hot(index, v_ref.shape[1]), preferred_element_type=F32).astype(BF16)
-
-
-def select_keep_kernel(index_ref, v_ref, send_ref, keep_ref, pay_ref):
-    chip, core = position()
-    index = jnp.where(chip == 0, index_ref[0:1], index_ref[1:2])
-    keep_ref[...] = jnp.dot(v_ref[...], one_hot(index, v_ref.shape[1]), preferred_element_type=F32).astype(BF16)
-
-    @pl.when(core == 0)
-    def _():
-        pay_ref[...] = send_ref[...]
-
-    @pl.when(core == 1)
-    def _():
-        pay_ref[...] = keep_ref[...]
-
-
 def split_upper(total_ref, halves, core, base, mine_ref, give_ref):
     for turn in range(2):
         @pl.when(core == turn)
@@ -180,7 +176,9 @@
     return step // 2
 
 
-def near_kernel(halves, x_ref, y_ref, keep_ref, send_ref, cross_ref, mine_ref, give_ref, main_ref, side_ref):
+def near_kernel(
+    halves, x_ref, y_ref, keep_ref, send_ref, keep_got_ref, send_got_ref, mine_ref, give_ref, main_ref, side_ref
+):
     step = pl.program_id(0)
     chip, core = position()
     unit = near_unit(step)
@@ -198,7 +196,10 @@
         u = (u * scale).astype(BF16)
         total_ref[...] += lax.dot_general(left_ref[rows, :], u, TN, preferred_element_type=F32)
 
-    for main_side, sel_ref, total_ref in ((True, keep_ref, main_ref), (False, send_ref, side_ref)):
+    for main_side, sel_ref, cross_ref, total_ref in (
+        (True, keep_ref, keep_got_ref, main_ref),
+        (False, send_ref, send_got_ref, side_ref),
+    ):
         for here in range(2):
             z_ref = x_ref if (here == 0) == main_side else y_ref
             at = (is_main == main_side) & (chip == here)
@@ -212,7 +213,7 @@
         split_upper(main_ref, halves, core, half, mine_ref, give_ref)
 
 
-def near(halves, x, y, keep, send, cross):
+def near(halves, x, y, keep, send, keep_got, send_got):
     depth, size = keep.shape
     tile = depth // 2
 
@@ -240,10 +241,8 @@
         in_specs=[
             pl.BlockSpec((tile, depth), reads(0)),
             pl.BlockSpec((tile, depth), reads(1)),
-            pl.BlockSpec(keep.shape, whole),
-            pl.BlockSpec(keep.shape, whole),
-            pl.BlockSpec(keep.shape, whole),
-        ],
+        ]
+        + [pl.BlockSpec(keep.shape, whole)] * 4,
         out_specs=(
             pl.BlockSpec(blocks, lambda step: (0, 0, 0)),
             pl.BlockSpec(blocks, lambda step: (0, 0, 0)),
@@ -253,7 +252,7 @@
             flops=6 * depth * size * (depth + size), bytes_accessed=6 * depth * (depth + size), transcendentals=0
         ),
         name="near",
-    )(x, y, keep, send, cross)
+    )(x, y, keep, send, keep_got, send_got)
 
 
 def far_products_kernel(x_ref, y_ref, keep_ref, give_ref, stay_ref):
@@ -299,10 +298,9 @@
     )(x, y, keep)
 
 
-def far_kernel(halves, sel_ref, own_ref, other_ref, mine_ref, give_ref, total_ref):
+def far_kernel(halves, sel_ref, both_ref, mine_ref, give_ref, total_ref):
     _, core = position()
-    both = (own_ref[...].astype(F32) + other_ref[...].astype(F32)).astype(BF16)
-    total_ref[...] = lax.dot_general(sel_ref[...], both, TN, preferred_element_type=F32)
+    total_ref[...] = lax.dot_general(sel_ref[...], both_ref[...], TN, preferred_element_type=F32)
     split_upper(total_ref, halves, core, 0, mine_ref, give_ref)
 
 
@@ -327,35 +325,33 @@
     half = len(halves[0])
     to_core = [(s, s ^ 1) for s in range(slabs)]
     to_chip = [(s, s ^ 2) for s in range(slabs)]
-    picked = jax.ShapeDtypeStruct((depth, size), BF16)
     blocks = jax.ShapeDtypeStruct((half, LANES, LANES), F32)
-
-    send = pl.pallas_call(
-        select_send_kernel, out_shape=picked, in_specs=[VMEM] * 2, out_specs=VMEM, name="select_send"
-    )(index, v)
+    chip, _ = position()
+    first, second = index
+
+    send = select_columns(v, jnp.where(chip == 0, second, first))
     far = lax.ppermute(send, "slab", to_chip)
-    keep, pay = pl.pallas_call(
-        select_keep_kernel, out_shape=(picked, picked), in_specs=[VMEM] * 3, out_specs=(VMEM, VMEM),
-        name="select_keep",
-    )(index, v, send)
-    cross = lax.ppermute(pay, "slab", to_core)
-    mine, give = near(halves, x, y, keep, send, cross)
+    send_got = lax.ppermute(send, "slab", [(s, d) for s, d in to_core if s < d])
+    keep = select_columns(v, jnp.where(chip == 0, first, second))
+    keep_got = lax.ppermute(keep, "slab", [(s, d) for s, d in to_core if s > d])
+    mine, give = near(halves, x, y, keep, send, keep_got, send_got)
     got = lax.ppermute(give, "slab", to_core)
+    side_sum = mine[:half] + got[:half]
+    early = lax.ppermute(side_sum, "slab", to_chip)
     far_give, far_stay = far_products(x, y, keep)
     far_got = lax.ppermute(far_give, "slab", to_core)
-    side_sum = mine[:half] + got[:half]
-    early = lax.ppermute(side_sum, "slab", to_chip)
+    both = (far_stay.astype(F32) + far_got.astype(F32)).astype(BF16)
     far_mine, far_give = pl.pallas_call(
         functools.partial(far_kernel, halves),
         out_shape=(blocks, blocks),
-        in_specs=[VMEM] * 3,
+        in_specs=[VMEM] * 2,
         out_specs=(VMEM, VMEM),
         scratch_shapes=[pltpu.VMEM((size, size), F32)],
         cost_estimate=pl.CostEstimate(
-            flops=2 * depth * size * size, bytes_accessed=6 * depth * size, transcendentals=0
+            flops=2 * depth * size * size, bytes_accessed=4 * depth * size, transcendentals=0
         ),
         name="far",
-    )(far, far_stay, far_got)
+    )(far, both)
     total = (mine[half:] + got[half:]) + early + (far_mine + lax.ppermute(far_give, "slab", to_core))
     schur = total * lax.ppermute(total, "slab", to_chip)
     other = lax.ppermute(schur, "slab", to_core)

time: 113 us -> 115 us (1.018)
  Pallas kernels: 49.6 us -> 36.1 us
  starting transfers between devices: 13.2 us -> 19.2 us
  waiting for transfers between devices: 30.6 us -> 35.1 us
  matrix products: 0 us -> 3.57 us
  other arithmetic: 2.95 us -> 5.62 us
  local copies, waits for them, and re-layouts: 4.27 us -> 2.77 us
    pallas_call x2 -> x0, Pallas kernels: 8.42 us -> none  [the longest x1 4.53 us: two_chips(): pl.pallas_call(select_keep_kernel, out_shape=(picked, picked), in_specs=[...]
    ppermute x1 -> x2, starting transfers between devices: 0.51 us -> 6.3 us  [the longest x1 5.01 us: two_chips(): send_got = lax.ppermute(send, 'slab', [(s, d) for s, d in to_core if s < d])]
    pallas_call x1, Pallas kernels: 19.5 us -> 13.9 us  [two_chips(): pl.pallas_call(functools.partial(factor_kernel, halves), out_shape=jax.Sh...]
    ppermute x1, waiting for transfers between devices: 4.49 us -> 9 us  [two_chips(): far = lax.ppermute(send, 'slab', to_chip)]
    dot_general x0 -> x2, matrix products: none -> 3.57 us  [select_columns(): return jnp.dot(v, hot, preferred_element_type=F32).astype(BF16)]
    convert_element_type x0 -> x1, other arithmetic: none -> 2.88 us  [two_chips(): both = (far_stay.astype(F32) + far_got.astype(F32)).astype(BF16)]
    unnamed x13, local copies, waits for them, and re-layouts: 3.71 us -> 2.21 us
  transfers between devices with their start and end apart: 9 -> 10, of which waited for: 5 -> 5; matrix products, arithmetic and copies ran while one was open for 1% -> 5% of each run, Pallas kernels for 19% -> 19%
where the time goes in v1:
time: 115 us; the launch traced here: 114 us
  Pallas kernels  36.1 us (31%)
  waiting for transfers between devices  35.1 us (31%)
  starting transfers between devices  19.2 us (17%)
  blocking collectives  12 us (10%)
  other arithmetic  5.62 us (5%)
  matrix products  3.57 us (3%)
  local copies, waits for them, and re-layouts  2.77 us (2%)
    pallas_call x1, Pallas kernels, two_chips(): pl.pallas_call(functools.partial(factor_kernel, halves), out_shape=jax.Sh...  13.9 us
    pallas_call x1, Pallas kernels, near(): pl.pallas_call(functools.partial(near_kernel, halves), out_shape=(jax.Sha...  12 us
    all_to_all x1, blocking collectives, place(): pieces = lax.all_to_all(pieces, 'blk', 0, 0)  12 us
    all_to_all x1, waiting for transfers between devices, place(): pieces = lax.all_to_all(pieces, 'blk', 0, 0)  9.19 us
    ppermute x1, waiting for transfers between devices, two_chips(): far = lax.ppermute(send, 'slab', to_chip)  9 us
    ppermute x1, waiting for transfers between devices, two_chips(): early = lax.ppermute(side_sum, 'slab', to_chip)  8.37 us
    ppermute x1, waiting for transfers between devices, two_chips(): schur = total * lax.ppermute(total, 'slab', to_chip)  7.51 us
    pallas_call x1, Pallas kernels, far_products(): pl.pallas_call(far_products_kernel, out_shape=(jax.ShapeDtypeStruct(keep....  6.64 us
  transfers between devices with their start and end apart: 10, of which 5 were waited for; matrix products, arithmetic and copies ran while one was open for 5% of the time, Pallas kernels for 19%

profile of v1, /device:TPU:0, one launch (start us, length us, event | category | flops | bytes accessed | tf_op | source)
XLA Modules:
  0.0 114.4 jit_solution(2545685099537327982)
XLA Ops:
  0.0 0.9 broadcast_select_fusion.1
  0.9 0.8 copy-done
  1.6 1.3 %fusion.13.keep_ref = bf16[1024,512]{1,0:T(8,128)(2,1)S(1)} fusion(bf16[1,1024,1024]{2,1,0:T(8,128)(2,1)S(1)} %copy-done, s32[512]{0:T(512)S(1)} %bitcast.30), kind=kOutput, calls=%fused_computation.11 | convolution fusion | flops 1074790400 | bytes 3147776 | tf_op jit(solution)/shard_map/dot_general | solution.py:309
  2.9 1.3 %collective-permute-start = (bf16[1024,512]{1,0:T(8,128)(2,1)S(1)}, bf16[1024,512]{1,0:T(8,128)(2,1)}, u32[]{:S(2)}, u32[]{:S(2)}) collective-permute-start(bf16[1024,512]{1,0:T(8,128)(2,1)S(1)} %fusion.13.keep_ref), channel_id=1, source_target_pairs={{1,0},{3,2},{5,4},{7,6},{9,8},{11,10},{13,12},{15,14},{17,16},{19,... | collective-permute-start | bytes 3145736 | tf_op jit(solution)/shard_map/ppermute | solution.py:336
  4.2 2.3 %fusion.10.send_ref = bf16[1024,512]{1,0:T(8,128)(2,1)} fusion(bf16[1,1024,1024]{2,1,0:T(8,128)(2,1)S(1)} %copy-done, s32[512]{0:T(512)S(1)} %bitcast.29), kind=kOutput, calls=%fused_computation.10 | convolution fusion | flops 1074790400 | bytes 3147776 | tf_op jit(solution)/shard_map/dot_general | solution.py:309
  6.5 5.0 %collective-permute-start.1 = (bf16[1024,512]{1,0:T(8,128)(2,1)}, bf16[1024,512]{1,0:T(8,128)(2,1)}, u32[]{:S(2)}, u32[]{:S(2)}) collective-permute-start(bf16[1024,512]{1,0:T(8,128)(2,1)} %fusion.10.send_ref), channel_id=1, source_target_pairs={{0,1},{2,3},{4,5},{6,7},{8,9},{10,11},{12,13},{14,15},{16,17},{18,... | collective-permute-start | bytes 3145736 | tf_op jit(solution)/shard_map/ppermute | solution.py:334
  11.5 6.6 %far_products.1 = (bf16[1024,512]{1,0:T(8,128)(2,1)}, bf16[1024,512]{1,0:T(8,128)(2,1)}) custom-call(bf16[4096,1024]{1,0:T(8,128)(2,1)} %bitcast.23, bf16[4096,1024]{1,0:T(8,128)(2,1)} %bitcast.25, bf16[1024,512]{1,0:T(8,128)(2,1)} %copy-done.1), custom_call_target="tpu_custom_call" | custom-call | flops 2147483648 | bytes 6291456 | tf_op jit(solution)/shard_map/far_products/pallas_call | solution.py:281
  18.2 3.0 %collective-permute-start.4 = (bf16[1024,512]{1,0:T(8,128)(2,1)}, bf16[1024,512]{1,0:T(8,128)(2,1)}, u32[]{:S(2)}, u32[]{:S(2)}) collective-permute-start(bf16[1024,512]{1,0:T(8,128)(2,1)} %fusion.10.send_ref), channel_id=1, source_target_pairs={{0,2},{1,3},{2,0},{3,1},{4,6},{5,7},{6,4},{7,5},{8,10},{9,11},{10,... | collective-permute-start | bytes 3145736 | tf_op jit(solution)/shard_map/ppermute | solution.py:333
  21.2 12.0 %near.1 = (f32[10,128,128]{2,1,0:T(8,128)}, f32[10,128,128]{2,1,0:T(8,128)}) custom-call(bf16[4096,1024]{1,0:T(8,128)(2,1)} %bitcast.24, bf16[4096,1024]{1,0:T(8,128)(2,1)} %bitcast.26, bf16[1024,512]{1,0:T(8,128)(2,1)} %copy-done.1, bf16[1024,512]{1,0:T(8,128)(2,1)} %fusion.10.send_ref, bf16[1024,512]{1,0:T(8,128)(2,1)} %collective-permute-done.keep_got_ref, ...), custom_call_target="tpu_custom_call" | custom-call | flops 4831838208 | bytes 9437184 | tf_op jit(solution)/shard_map/near/pallas_call | solution.py:237
  33.4 2.9 %add_convert_fusion.both_ref = bf16[1024,512]{1,0:T(8,128)(2,1)} fusion(bf16[1024,512]{1,0:T(8,128)(2,1)} %collective-permute-done.5, bf16[1024,512]{1,0:T(8,128)(2,1)} %get-tuple-element.15), kind=kLoop, calls=%fused_computation.5 | loop fusion | flops 2097152 | bytes 3145728 | tf_op jit(solution)/shard_map/convert_element_type | solution.py:343
  36.3 9.0 %collective-permute-done.4.sel_ref = bf16[1024,512]{1,0:T(8,128)(2,1)} collective-permute-done((bf16[1024,512]{1,0:T(8,128)(2,1)}, bf16[1024,512]{1,0:T(8,128)(2,1)}, u32[]{:S(2)}, u32[]{:S(2)}) %collective-permute-start.4) | collective-permute-done | bytes 1048608 | tf_op jit(solution)/shard_map/ppermute | solution.py:333
  45.3 3.5 %far.1 = (f32[5,128,128]{2,1,0:T(8,128)}, f32[5,128,128]{2,1,0:T(8,128)}) custom-call(bf16[1024,512]{1,0:T(8,128)(2,1)} %collective-permute-done.4.sel_ref, bf16[1024,512]{1,0:T(8,128)(2,1)} %add_convert_fusion.both_ref), custom_call_target="tpu_custom_call" | custom-call | flops 536870912 | bytes 2097152 | tf_op jit(solution)/shard_map/far/pallas_call | solution.py:344
  48.9 1.8 %collective-permute-start.3 = (f32[5,128,128]{2,1,0:T(8,128)S(1)}, f32[5,128,128]{2,1,0:T(8,128)S(1)}, u32[]{:S(2)}, u32[]{:S(2)}) collective-permute-start(f32[5,128,128]{2,1,0:T(8,128)S(1)} %slice_add_fusion), channel_id=1, source_target_pairs={{0,2},{1,3},{2,0},{3,1},{4,6},{5,7},{6,4},{7,5},{8,10},{9,11},{10,... | collective-permute-start | bytes 983048 | tf_op jit(solution)/shard_map/ppermute | solution.py:340
  50.7 8.4 %collective-permute-done.3 = f32[5,128,128]{2,1,0:T(8,128)S(1)} collective-permute-done((f32[5,128,128]{2,1,0:T(8,128)S(1)}, f32[5,128,128]{2,1,0:T(8,128)S(1)}, u32[]{:S(2)}, u32[]{:S(2)}) %collective-permute-start.3) | collective-permute-done | bytes 327712 | tf_op jit(solution)/shard_map/ppermute | solution.py:340
  59.0 1.1 fusion.19
  60.1 1.8 %collective-permute-start.7 = (f32[5,128,128]{2,1,0:T(8,128)S(1)}, f32[5,128,128]{2,1,0:T(8,128)S(1)}, u32[]{:S(2)}, u32[]{:S(2)}) collective-permute-start(f32[5,128,128]{2,1,0:T(8,128)S(1)} %fusion.19), channel_id=1, source_target_pairs={{0,2},{1,3},{2,0},{3,1},{4,6},{5,7},{6,4},{7,5},{8,10},{9,11},{10,... | collective-permute-start | bytes 983048 | tf_op jit(solution)/shard_map/ppermute | solution.py:356
  61.9 7.5 %collective-permute-done.7 = f32[5,128,128]{2,1,0:T(8,128)S(1)} collective-permute-done((f32[5,128,128]{2,1,0:T(8,128)S(1)}, f32[5,128,128]{2,1,0:T(8,128)S(1)}, u32[]{:S(2)}, u32[]{:S(2)}) %collective-permute-start.7) | collective-permute-done | bytes 327712 | tf_op jit(solution)/shard_map/ppermute | solution.py:356
  70.2 1.0 collective-permute-done.8.theirs_ref
  71.2 0.7 copy-done.4
  71.9 13.9 %factor.1 = f32[128,512]{1,0:T(8,128)} custom-call(s32[8]{0:T(128)} %orders_ref.1, f32[5,128,128]{2,1,0:T(8,128)} %copy-done.2, f32[5,128,128]{2,1,0:T(8,128)} %copy-done.4), custom_call_target="tpu_custom_call" | custom-call | tf_op jit(solution)/shard_map/factor/pallas_call | solution.py:358
  85.8 6.0 %all-to-all-start = ((f32[8,16,512]{2,1,0:T(8,128)}), f32[8,16,512]{2,1,0:T(8,128)S(1)}, u32[]{:S(2)}, u32[]{:S(2)}) async-start(f32[8,16,512]{2,1,0:T(8,128)} %bitcast.27), calls=%async_computation | async-start | bytes 524288 | tf_op jit(solution)/shard_map/all_to_all | solution.py:315
  91.9 9.2 %all-to-all-done = f32[8,16,512]{2,1,0:T(8,128)S(1)} async-done(((f32[8,16,512]{2,1,0:T(8,128)}), f32[8,16,512]{2,1,0:T(8,128)S(1)}, u32[]{:S(2)}, u32[]{:S(2)}) %all-to-all-start) | async-done | bytes 262176 | tf_op jit(solution)/shard_map/all_to_all | solution.py:315
  101.7 12.0 %all_to_all.10 = f32[8,16,512]{2,1,0:T(8,128)S(1)} all-to-all(f32[8,16,512]{2,1,0:T(8,128)S(1)} %broadcast_select_fusion), channel_id=1, replica_groups=mesh['blk'=8,'slab'=4] {'blk'}, dimensions={0} | all-to-all | bytes 524288 | tf_op jit(solution)/shard_map/all_to_all | solution.py:317
  113.7 0.7 copy.14
  (27 shorter events, 1.7 us)
Async XLA Ops:
  0.0 1.6 %copy-start = (bf16[1,1024,1024]{2,1,0:T(8,128)(2,1)S(1)}, bf16[1,1024,1024]{2,1,0:T(8,128)(2,1)}, u32[]{:S(2)}) copy-start(bf16[1,1024,1024]{2,1,0:T(8,128)(2,1)} %param.8) | copy-start | bytes 6291460
  2.9 3.6 %copy-start.1 = (bf16[1024,512]{1,0:T(8,128)(2,1)}, bf16[1024,512]{1,0:T(8,128)(2,1)S(1)}, u32[]{:S(2)}) copy-start(bf16[1024,512]{1,0:T(8,128)(2,1)S(1)} %fusion.13.keep_ref) | copy-start | bytes 3145732
  2.9 18.2 %collective-permute-start = (bf16[1024,512]{1,0:T(8,128)(2,1)S(1)}, bf16[1024,512]{1,0:T(8,128)(2,1)}, u32[]{:S(2)}, u32[]{:S(2)}) collective-permute-start(bf16[1024,512]{1,0:T(8,128)(2,1)S(1)} %fusion.13.keep_ref), channel_id=1, source_target_pairs={{1,0},{3,2},{5,4},{7,6},{9,8},{11,10},{13,12},{15,14},{17,16},{19,... | collective-permute-start | bytes 3145736 | tf_op jit(solution)/shard_map/ppermute | solution.py:336
  6.5 14.6 %collective-permute-start.1 = (bf16[1024,512]{1,0:T(8,128)(2,1)}, bf16[1024,512]{1,0:T(8,128)(2,1)}, u32[]{:S(2)}, u32[]{:S(2)}) collective-permute-start(bf16[1024,512]{1,0:T(8,128)(2,1)} %fusion.10.send_ref), channel_id=1, source_target_pairs={{0,1},{2,3},{4,5},{6,7},{8,9},{10,11},{12,13},{14,15},{16,17},{18,... | collective-permute-start | bytes 3145736 | tf_op jit(solution)/shard_map/ppermute | solution.py:334
  18.2 15.2 %collective-permute-start.5 = (bf16[1024,512]{1,0:T(8,128)(2,1)}, bf16[1024,512]{1,0:T(8,128)(2,1)}, u32[]{:S(2)}, u32[]{:S(2)}) collective-permute-start(bf16[1024,512]{1,0:T(8,128)(2,1)} %get-tuple-element.16), channel_id=1, source_target_pairs={{0,1},{1,0},{2,3},{3,2},{4,5},{5,4},{6,7},{7,6},{8,9},{9,8},{10,11... | collective-permute-start | bytes 3145736 | tf_op jit(solution)/shard_map/ppermute | solution.py:342
  18.2 27.1 %collective-permute-start.4 = (bf16[1024,512]{1,0:T(8,128)(2,1)}, bf16[1024,512]{1,0:T(8,128)(2,1)}, u32[]{:S(2)}, u32[]{:S(2)}) collective-permute-start(bf16[1024,512]{1,0:T(8,128)(2,1)} %fusion.10.send_ref), channel_id=1, source_target_pairs={{0,2},{1,3},{2,0},{3,1},{4,6},{5,7},{6,4},{7,5},{8,10},{9,11},{10,... | collective-permute-start | bytes 3145736 | tf_op jit(solution)/shard_map/ppermute | solution.py:333
  33.2 15.6 %collective-permute-start.2 = (f32[10,128,128]{2,1,0:T(8,128)}, f32[10,128,128]{2,1,0:T(8,128)S(1)}, u32[]{:S(2)}, u32[]{:S(2)}) collective-permute-start(f32[10,128,128]{2,1,0:T(8,128)} %get-tuple-element.14), channel_id=1, source_target_pairs={{0,1},{1,0},{2,3},{3,2},{4,5},{5,4},{6,7},{7,6},{8,9},{9,8},{10,11... | collective-permute-start | bytes 1966088 | tf_op jit(solution)/shard_map/ppermute | solution.py:338
  33.4 15.4 %copy-start.3 = (f32[10,128,128]{2,1,0:T(8,128)S(1)}, f32[10,128,128]{2,1,0:T(8,128)}, u32[]{:S(2)}) copy-start(f32[10,128,128]{2,1,0:T(8,128)} %get-tuple-element.13) | copy-start | bytes 1966084
  48.8 20.8 %copy-start.5 = (s32[8]{0:T(128)S(1)}, s32[8]{0:T(128)}, u32[]{:S(2)}) copy-start(s32[8]{0:T(128)} %param.11) | copy-start | bytes 100
  48.8 1.9 %collective-permute-start.6 = (f32[5,128,128]{2,1,0:T(8,128)}, f32[5,128,128]{2,1,0:T(8,128)S(1)}, u32[]{:S(2)}, u32[]{:S(2)}) collective-permute-start(f32[5,128,128]{2,1,0:T(8,128)} %get-tuple-element.18), channel_id=1, source_target_pairs={{0,1},{1,0},{2,3},{3,2},{4,5},{5,4},{6,7},{7,6},{8,9},{9,8},{10,11... | collective-permute-start | bytes 983048 | tf_op jit(solution)/shard_map/ppermute | solution.py:355
  48.9 10.2 %collective-permute-start.3 = (f32[5,128,128]{2,1,0:T(8,128)S(1)}, f32[5,128,128]{2,1,0:T(8,128)S(1)}, u32[]{:S(2)}, u32[]{:S(2)}) collective-permute-start(f32[5,128,128]{2,1,0:T(8,128)S(1)} %slice_add_fusion), channel_id=1, source_target_pairs={{0,2},{1,3},{2,0},{3,1},{4,6},{5,7},{6,4},{7,5},{8,10},{9,11},{10,... | collective-permute-start | bytes 983048 | tf_op jit(solution)/shard_map/ppermute | solution.py:340
  60.1 9.3 %collective-permute-start.7 = (f32[5,128,128]{2,1,0:T(8,128)S(1)}, f32[5,128,128]{2,1,0:T(8,128)S(1)}, u32[]{:S(2)}, u32[]{:S(2)}) collective-permute-start(f32[5,128,128]{2,1,0:T(8,128)S(1)} %fusion.19), channel_id=1, source_target_pairs={{0,2},{1,3},{2,0},{3,1},{4,6},{5,7},{6,4},{7,5},{8,10},{9,11},{10,... | collective-permute-start | bytes 983048 | tf_op jit(solution)/shard_map/ppermute | solution.py:356
  69.5 1.7 %copy-start.2 = (f32[5,128,128]{2,1,0:T(8,128)}, f32[5,128,128]{2,1,0:T(8,128)S(1)}, u32[]{:S(2)}) copy-start(f32[5,128,128]{2,1,0:T(8,128)S(1)} %mul.3.mine_ref) | copy-start | bytes 983044
  69.5 1.7 %collective-permute-start.8 = (f32[5,128,128]{2,1,0:T(8,128)S(1)}, f32[5,128,128]{2,1,0:T(8,128)S(1)}, u32[]{:S(2)}, u32[]{:S(2)}) collective-permute-start(f32[5,128,128]{2,1,0:T(8,128)S(1)} %mul.3.mine_ref), channel_id=1, source_target_pairs={{0,1},{1,0},{2,3},{3,2},{4,5},{5,4},{6,7},{7,6},{8,9},{9,8},{10,11... | collective-permute-start | bytes 983048 | tf_op jit(solution)/shard_map/ppermute | solution.py:357
  71.2 0.7 copy-start.4
  85.8 15.3 %all-to-all-start = ((f32[8,16,512]{2,1,0:T(8,128)}), f32[8,16,512]{2,1,0:T(8,128)S(1)}, u32[]{:S(2)}, u32[]{:S(2)}) async-start(f32[8,16,512]{2,1,0:T(8,128)} %bitcast.27), calls=%async_computation | async-start | bytes 524288 | tf_op jit(solution)/shard_map/all_to_all | solution.py:315

commit v2 on v1

--- a/solution.py
+++ b/solution.py
@@ -13,9 +13,12 @@
 LANES = 128
 MICRO = 8
 GROUP = 4
+AHEAD = 1
 VMEM = pl.BlockSpec(memory_space=pltpu.VMEM)
 SMEM = pl.BlockSpec(memory_space=pltpu.SMEM)
+ANY = pl.BlockSpec(memory_space=pl.ANY)
 TN = (((0,), (0,)), ((), ()))
+NT = (((1,), (1,)), ((), ()))
 
 
 def dot_f32(a, b, dims):
@@ -71,7 +74,7 @@
         a_ref[here, span] = jnp.where(lane >= sub + base, packed, 0.0)
         group_end = (m // GROUP + 1) * GROUP
         cols = None
-        for later in range(m + 1, min(group_end + 1, count)):
+        for later in range(m + 1, min(group_end + AHEAD, count)):
             there = slice(start + MICRO * later, start + MICRO * later + MICRO)
             rest = a_ref[there, span]
             head = rest[:, :LANES]
@@ -88,9 +91,9 @@
             for k in range(MICRO):
                 rest = by_tile(lambda x, u: x - part[k] * u, rest, wide[k])
             a_ref[there, span] = rest
-        if m + 1 == group_end and group_end + 1 < count:
+        if m + 1 == group_end and group_end + AHEAD < count:
             done = a_ref[start + MICRO * (group_end - GROUP) : start + MICRO * group_end, span]
-            first = MICRO * (group_end + 1)
+            first = MICRO * (group_end + AHEAD)
             there = slice(start + first, start + LANES)
             a_ref[there, span] = a_ref[there, span] - dot_f32(done[:, :LANES], done, TN)[first:]
 
@@ -161,7 +164,7 @@
     own_rows(a_ref, out_ref, lax.axis_index("slab") * out_ref.shape[0])
 
 
-def split_upper(total_ref, halves, core, base, mine_ref, give_ref):
+def split_upper(total_ref, halves, core, mine_ref, give_ref):
     for turn in range(2):
         @pl.when(core == turn)
         def _():
@@ -169,144 +172,121 @@
                 for t, (i, k) in enumerate(half):
                     i, k = i * LANES, k * LANES
                     mirror = total_ref[k : k + LANES, i : i + LANES].T
-                    ref[base + t] = total_ref[i : i + LANES, k : k + LANES] + mirror
-
-
-def near_unit(step):
-    return step // 2
+                    ref[t] = total_ref[i : i + LANES, k : k + LANES] + mirror
+
+
+def fetch(z_refs, use_x, slab, held_ref, sems, first):
+    half = held_ref.shape[1]
+    waits = []
+    for t in range(2):
+        rows = pl.ds(pl.multiple_of((slab * 2 + t) * half, half), half)
+        copies = [
+            pltpu.make_async_copy(z_ref.at[rows], held_ref.at[first + t], sems.at[first + t]) for z_ref in z_refs
+        ]
+        pl.when(use_x)(copies[0].start)
+        pl.when(jnp.logical_not(use_x))(copies[1].start)
+        waits.append(copies[0].wait)
+    return waits
 
 
 def near_kernel(
-    halves, x_ref, y_ref, keep_ref, send_ref, keep_got_ref, send_got_ref, mine_ref, give_ref, main_ref, side_ref
+    halves, x_ref, y_ref, keep_ref, send_ref, cross_ref,
+    side_mine_ref, side_give_ref, main_mine_ref, main_give_ref, main_ref, side_ref, held_ref, sems,
 ):
-    step = pl.program_id(0)
     chip, core = position()
-    unit = near_unit(step)
-    tile = x_ref.shape[0]
-    rows = pl.ds((step % 2) * tile, tile)
-    is_main = (unit == 0) | ((unit == 2) & (core == 0))
-
-    @pl.when(step == 0)
-    def _():
-        main_ref[...] = jnp.zeros_like(main_ref)
-        side_ref[...] = jnp.zeros_like(side_ref)
-
-    def add(z_ref, sel_ref, left_ref, scale, total_ref):
-        u = jnp.dot(z_ref[...], sel_ref[...], preferred_element_type=F32)
-        u = (u * scale).astype(BF16)
-        total_ref[...] += lax.dot_general(left_ref[rows, :], u, TN, preferred_element_type=F32)
-
-    for main_side, sel_ref, cross_ref, total_ref in (
-        (True, keep_ref, keep_got_ref, main_ref),
-        (False, send_ref, send_got_ref, side_ref),
-    ):
-        for here in range(2):
-            z_ref = x_ref if (here == 0) == main_side else y_ref
-            at = (is_main == main_side) & (chip == here)
-            pl.when(at & (unit != 2))(lambda: add(z_ref, sel_ref, sel_ref, 0.5, total_ref))
-            pl.when(at & (unit == 2))(lambda: add(z_ref, sel_ref, cross_ref, 1.0, total_ref))
-
-    @pl.when(step == pl.num_programs(0) - 1)
-    def _():
-        half = len(halves[0])
-        split_upper(side_ref, halves, core, 0, mine_ref, give_ref)
-        split_upper(main_ref, halves, core, half, mine_ref, give_ref)
-
-
-def near(halves, x, y, keep, send, keep_got, send_got):
-    depth, size = keep.shape
-    tile = depth // 2
-
-    def reads(matrix):
-        def index(step):
-            chip, core = position()
-            unit = near_unit(step)
-            is_main = (unit == 0) | ((unit == 2) & (core == 0))
-            mine = is_main == (chip == matrix)
-            own, other = (chip * 2 + core) * 2, (chip * 2 + 1 - core) * 2
-            late = jnp.where((core == 0) == (chip == matrix), other, own + 1)
-            early = jnp.where(chip == matrix, own, own)
-            row = jnp.where(unit == 2, other, own) + step % 2
-            after = jnp.where(step >= 2, late, early)
-            return jnp.where(mine, row, after), 0
-
-        return index
-
-    whole = lambda step: (0, 0)
-    blocks = (2 * len(halves[0]), LANES, LANES)
+    own, other = chip * 2 + core, chip * 2 + 1 - core
+    half = held_ref.shape[1]
+    waits = (
+        fetch((x_ref, y_ref), chip == 0, own, held_ref, sems, 0)
+        + fetch((x_ref, y_ref), chip == 1, own, held_ref, sems, 2)
+        + fetch((x_ref, y_ref), chip == core, other, held_ref, sems, 4)
+    )
+
+    def add(t, sel_ref, left_ref, scale, total_ref, fresh):
+        u = lax.dot_general(held_ref[t], sel_ref[...], NT, preferred_element_type=F32)
+        left = left_ref[:, t % 2 * half : (t % 2 + 1) * half]
+        part = jnp.dot(left, (u * scale).astype(BF16), preferred_element_type=F32)
+        total_ref[...] = part if fresh else total_ref[...] + part
+
+    for t, wait in enumerate(waits):
+        wait()
+        if t < 2:
+            add(t, keep_ref, keep_ref, 0.5, main_ref, t == 0)
+        elif t < 4:
+            add(t, send_ref, send_ref, 0.5, side_ref, t == 2)
+        else:
+            pl.when(core == 0)(functools.partial(add, t, keep_ref, cross_ref, 1.0, main_ref, False))
+            pl.when(core == 1)(functools.partial(add, t, send_ref, cross_ref, 1.0, side_ref, False))
+    split_upper(side_ref, halves, core, side_mine_ref, side_give_ref)
+    split_upper(main_ref, halves, core, main_mine_ref, main_give_ref)
+
+
+def in_hbm(z):
+    return pltpu.with_memory_space_constraint(z, pltpu.HBM)
+
+
+def near(halves, x, y, keep, send, cross):
+    size, depth = keep.shape
+    blocks = (len(halves[0]), LANES, LANES)
     return pl.pallas_call(
         functools.partial(near_kernel, halves),
-        out_shape=(jax.ShapeDtypeStruct(blocks, F32), jax.ShapeDtypeStruct(blocks, F32)),
-        grid=(6,),
-        in_specs=[
-            pl.BlockSpec((tile, depth), reads(0)),
-            pl.BlockSpec((tile, depth), reads(1)),
-        ]
-        + [pl.BlockSpec(keep.shape, whole)] * 4,
-        out_specs=(
-            pl.BlockSpec(blocks, lambda step: (0, 0, 0)),
-            pl.BlockSpec(blocks, lambda step: (0, 0, 0)),
-        ),
-        scratch_shapes=[pltpu.VMEM((size, size), F32), pltpu.VMEM((size, size), F32)],
+        out_shape=(jax.ShapeDtypeStruct(blocks, F32),) * 4,
+        in_specs=[ANY, ANY, VMEM, VMEM, VMEM],
+        out_specs=(VMEM,) * 4,
+        scratch_shapes=[
+            pltpu.VMEM((size, size), F32),
+            pltpu.VMEM((size, size), F32),
+            pltpu.VMEM((6, depth // 2, depth), BF16),
+            pltpu.SemaphoreType.DMA((6,)),
+        ],
         cost_estimate=pl.CostEstimate(
             flops=6 * depth * size * (depth + size), bytes_accessed=6 * depth * (depth + size), transcendentals=0
         ),
         name="near",
-    )(x, y, keep, send, keep_got, send_got)
-
-
-def far_products_kernel(x_ref, y_ref, keep_ref, give_ref, stay_ref):
-    chip, _ = position()
-    step = pl.program_id(0)
-    for here, z_ref in ((0, x_ref), (1, y_ref)):
-        for turn, out_ref in ((0, give_ref), (1, stay_ref)):
-            @pl.when((chip == here) & (step // 2 == turn))
-            def _():
-                out_ref[...] = jnp.dot(z_ref[...], keep_ref[...], preferred_element_type=F32).astype(BF16)
-
-
-def far_products(x, y, keep):
-    depth, size = keep.shape
-    tile = depth // 2
-
-    def reads(matrix):
-        def index(step):
-            chip, core = position()
-            holder = jnp.where(step < 2, 1 - core, core)
-            row = ((1 - chip) * 2 + holder) * 2 + step % 2
-            return jnp.where(chip == matrix, row, 0), 0
-
-        return index
-
+        compiler_params=pltpu.CompilerParams(vmem_limit_bytes=20 << 20),
+    )(in_hbm(x), in_hbm(y), keep, send, cross)
+
+
+def far_product_kernel(x_ref, y_ref, keep_ref, *refs):
+    got_ref, (out_ref, held_ref, sems) = (refs[0] if len(refs) == 4 else None), refs[-3:]
+    chip, core = position()
+    half = held_ref.shape[1]
+    holder = 1 - core if got_ref is None else core
+    waits = fetch((x_ref, y_ref), chip == 0, (1 - chip) * 2 + holder, held_ref, sems, 0)
+    for t, wait in enumerate(waits):
+        wait()
+        rows = slice(t * half, t * half + half)
+        u = lax.dot_general(held_ref[t], keep_ref[...], NT, preferred_element_type=F32)
+        if got_ref is not None:
+            u = u + got_ref[rows, :].astype(F32)
+        out_ref[rows, :] = u.astype(BF16)
+
+
+def far_product(x, y, keep, *got):
+    size, depth = keep.shape
     return pl.pallas_call(
-        far_products_kernel,
-        out_shape=(jax.ShapeDtypeStruct(keep.shape, BF16), jax.ShapeDtypeStruct(keep.shape, BF16)),
-        grid=(4,),
-        in_specs=[
-            pl.BlockSpec((tile, depth), reads(0)),
-            pl.BlockSpec((tile, depth), reads(1)),
-            pl.BlockSpec(keep.shape, lambda step: (0, 0)),
-        ],
-        out_specs=(
-            pl.BlockSpec((tile, size), lambda step: (jnp.minimum(step, 1), 0)),
-            pl.BlockSpec((tile, size), lambda step: (jnp.maximum(step - 2, 0), 0)),
+        far_product_kernel,
+        out_shape=jax.ShapeDtypeStruct((depth, size), BF16),
+        in_specs=[ANY, ANY, VMEM] + [VMEM] * len(got),
+        out_specs=VMEM,
+        scratch_shapes=[pltpu.VMEM((2, depth // 2, depth), BF16), pltpu.SemaphoreType.DMA((2,))],
+        cost_estimate=pl.CostEstimate(
+            flops=2 * depth * depth * size, bytes_accessed=2 * depth * (depth + 2 * size), transcendentals=0
         ),
-        cost_estimate=pl.CostEstimate(
-            flops=4 * depth * depth * size, bytes_accessed=4 * depth * (depth + size), transcendentals=0
-        ),
-        name="far_products",
-    )(x, y, keep)
+        name="far_product",
+        compiler_params=pltpu.CompilerParams(vmem_limit_bytes=20 << 20),
+    )(in_hbm(x), in_hbm(y), keep, *got)
 
 
 def far_kernel(halves, sel_ref, both_ref, mine_ref, give_ref, total_ref):
     _, core = position()
-    total_ref[...] = lax.dot_general(sel_ref[...], both_ref[...], TN, preferred_element_type=F32)
-    split_upper(total_ref, halves, core, 0, mine_ref, give_ref)
+    total_ref[...] = jnp.dot(sel_ref[...], both_ref[...], preferred_element_type=F32)
+    split_upper(total_ref, halves, core, mine_ref, give_ref)
 
 
 def select_columns(v, index):
-    hot = (lax.broadcasted_iota(jnp.int32, (v.shape[1], index.shape[0]), 0) == index[None, :]).astype(BF16)
-    return jnp.dot(v, hot, preferred_element_type=F32).astype(BF16)
+    hot = (index[:, None] == lax.broadcasted_iota(jnp.int32, (index.shape[0], v.shape[1]), 1)).astype(BF16)
+    return lax.dot_general(hot, v, NT, preferred_element_type=F32).astype(BF16)
 
 
 def place(own, dest, groups):
@@ -326,21 +306,20 @@
     to_core = [(s, s ^ 1) for s in range(slabs)]
     to_chip = [(s, s ^ 2) for s in range(slabs)]
     blocks = jax.ShapeDtypeStruct((half, LANES, LANES), F32)
-    chip, _ = position()
+    chip, core = position()
     first, second = index
 
-    send = select_columns(v, jnp.where(chip == 0, second, first))
+    send = lax.optimization_barrier(select_columns(v, jnp.where(chip == 0, second, first)))
     far = lax.ppermute(send, "slab", to_chip)
-    send_got = lax.ppermute(send, "slab", [(s, d) for s, d in to_core if s < d])
     keep = select_columns(v, jnp.where(chip == 0, first, second))
-    keep_got = lax.ppermute(keep, "slab", [(s, d) for s, d in to_core if s > d])
-    mine, give = near(halves, x, y, keep, send, keep_got, send_got)
+    cross = lax.ppermute(jnp.where(core == 0, send, keep), "slab", to_core)
+    give = far_product(x, y, keep)
     got = lax.ppermute(give, "slab", to_core)
-    side_sum = mine[:half] + got[:half]
+    side_mine, side_give, main_mine, main_give = near(halves, x, y, keep, send, cross)
+    side_sum = side_mine + lax.ppermute(side_give, "slab", to_core)
     early = lax.ppermute(side_sum, "slab", to_chip)
-    far_give, far_stay = far_products(x, y, keep)
-    far_got = lax.ppermute(far_give, "slab", to_core)
-    both = (far_stay.astype(F32) + far_got.astype(F32)).astype(BF16)
+    both = far_product(x, y, keep, got)
+    main_sum = main_mine + lax.ppermute(main_give, "slab", to_core)
     far_mine, far_give = pl.pallas_call(
         functools.partial(far_kernel, halves),
         out_shape=(blocks, blocks),
@@ -351,8 +330,9 @@
             flops=2 * depth * size * size, bytes_accessed=4 * depth * size, transcendentals=0
         ),
         name="far",
+        compiler_params=pltpu.CompilerParams(vmem_limit_bytes=8 << 20),
     )(far, both)
-    total = (mine[half:] + got[half:]) + early + (far_mine + lax.ppermute(far_give, "slab", to_core))
+    total = main_sum + early + (far_mine + lax.ppermute(far_give, "slab", to_core))
     schur = total * lax.ppermute(total, "slab", to_chip)
     other = lax.ppermute(schur, "slab", to_core)
     own = pl.pallas_call(
@@ -362,6 +342,7 @@
         out_specs=VMEM,
         scratch_shapes=[pltpu.VMEM((size, size), F32)],
         name="factor",
+        compiler_params=pltpu.CompilerParams(vmem_limit_bytes=8 << 20),
     )(orders, schur, other)
     return place(own, dest, groups)
 
@@ -377,9 +358,9 @@
 
     def pairing(z, index):
         picked = select_columns(v, index)
-        every = lax.all_gather(picked, "slab", axis=0, tiled=True)
-        c = lax.dot_general(every, z, TN, preferred_element_type=F32).astype(BF16)
-        return jnp.dot(c, picked, preferred_element_type=F32)
+        every = lax.all_gather(picked, "slab", axis=1, tiled=True)
+        c = jnp.dot(every, z, preferred_element_type=F32).astype(BF16)
+        return lax.dot_general(c, picked, NT, preferred_element_type=F32)
 
     both = jnp.concatenate([pairing(x, first), pairing(y, second)], axis=1)
     both = lax.psum_scatter(both, "slab", scatter_dimension=0, tiled=True)
@@ -397,6 +378,7 @@
         out_specs=VMEM,
         scratch_shapes=[pltpu.VMEM((size, size), F32)],
         name="factor",
+        compiler_params=pltpu.CompilerParams(vmem_limit_bytes=8 << 20),
     )(whole)
     return place(own, dest, groups)
 

time: 115 us -> 98.6 us (0.86)
  Pallas kernels: 36.1 us -> 27.9 us
  starting transfers between devices: 19.2 us -> 14 us
  other arithmetic: 5.62 us -> 1.75 us
  waiting for transfers between devices: 35.1 us -> 37.9 us
    ppermute x3, starting transfers between devices: 6.31 us -> 1.13 us  [the longest x1 0.56 us: two_chips(): cross = lax.ppermute(jnp.where(core == 0, send, keep), 'slab', to_core)]
    pallas_call x1, Pallas kernels: 12 us -> 8.23 us  [near(): pl.pallas_call(functools.partial(near_kernel, halves), out_shape=(jax.Sha...]
    convert_element_type x1 -> x0, other arithmetic: 2.88 us -> none  [two_chips(): both = (far_stay.astype(F32) + far_got.astype(F32)).astype(BF16)]
    ppermute x1, waiting for transfers between devices: 9 us -> 11.8 us  [two_chips(): far = lax.ppermute(send, 'slab', to_chip)]
    pallas_call x1, Pallas kernels: 3.51 us -> 0.91 us  [two_chips(): pl.pallas_call(functools.partial(far_kernel, halves), out_shape=(blocks,...]
    pallas_call x1 -> x2, Pallas kernels: 6.64 us -> 5.46 us  [far_product(): pl.pallas_call(far_product_kernel, out_shape=jax.ShapeDtypeStruct((depth,...]
  transfers between devices with their start and end apart: 10 -> 10, of which waited for: 5 -> 5; matrix products, arithmetic and copies ran while one was open for 5% -> 1% of each run, Pallas kernels for 19% -> 15%
where the time goes in v2:
time: 98.6 us; the launch traced here: 98.3 us
  waiting for transfers between devices  37.9 us (38%)
  Pallas kernels  27.9 us (28%)
  starting transfers between devices  14 us (14%)
  blocking collectives  12 us (12%)
  matrix products  2.58 us (3%)
  local copies, waits for them, and re-layouts  2.04 us (2%)
  other arithmetic  1.75 us (2%)
    pallas_call x1, Pallas kernels, two_chips(): pl.pallas_call(functools.partial(factor_kernel, halves), out_shape=jax.Sh...  13.3 us
    all_to_all x1, blocking collectives, place(): pieces = lax.all_to_all(pieces, 'blk', 0, 0)  12 us
    ppermute x1, waiting for transfers between devices, two_chips(): far = lax.ppermute(send, 'slab', to_chip)  11.8 us
    all_to_all x1, waiting for transfers between devices, place(): pieces = lax.all_to_all(pieces, 'blk', 0, 0)  9.17 us
    ppermute x1, waiting for transfers between devices, two_chips(): early = lax.ppermute(side_sum, 'slab', to_chip)  8.35 us
    pallas_call x1, Pallas kernels, near(): pl.pallas_call(functools.partial(near_kernel, halves), out_shape=(jax.Sha...  8.23 us
    ppermute x1, waiting for transfers between devices, two_chips(): schur = total * lax.ppermute(total, 'slab', to_chip)  7.5 us
    all_to_all x1, starting transfers between devices, place(): pieces = lax.all_to_all(pieces, 'blk', 0, 0)  6.03 us
  transfers between devices with their start and end apart: 10, of which 5 were waited for; matrix products, arithmetic and copies ran while one was open for 1% of the time, Pallas kernels for 15%

profile of v2, /device:TPU:0, one launch (start us, length us, event | category | flops | bytes accessed | tf_op | source)
XLA Modules:
  0.0 98.3 jit_solution(9939309626668487932)
XLA Ops:
  0.0 0.9 broadcast_select_fusion.3
  0.9 0.8 copy-done
  1.6 1.3 %fusion.7.send_ref = bf16[512,1024]{1,0:T(8,128)(2,1)S(1)} fusion(bf16[1,1024,1024]{2,1,0:T(8,128)(2,1)S(1)} %copy-done, s32[512]{0:T(512)S(1)} %bitcast.25), kind=kOutput, calls=%fused_computation.8 | convolution fusion | flops 1074790400 | bytes 3147776 | tf_op jit(solution)/shard_map/dot_general | solution.py:289
  2.9 1.3 %broadcast_select_fusion = (bf16[512,1024]{1,0:T(8,128)(2,1)S(1)}, bf16[512,1024]{1,0:T(8,128)(2,1)S(1)}) fusion(bf16[512,1024]{1,0:T(8,128)(2,1)S(1)} %fusion.7.send_ref, pred[]{:T(512)S(6)} %eq.48, bf16[1,1024,1024]{2,1,0:T(8,128)(2,1)S(1)} %copy-done, s32[512]{0:T(512)S(1)} %bitcast.24), kind=kOutput, calls=%fused_computation.11 | convolution fusion | flops 1075314688 | bytes 5244929 | tf_op jit(solution)/shard_map/dot_general | solution.py:289
  4.2 0.6 collective-permute-start
  4.8 2.7 %far_product.2 = bf16[1024,512]{1,0:T(8,128)(2,1)S(1)} custom-call(bf16[4096,1024]{1,0:T(8,128)(2,1)} %bitcast.17, bf16[4096,1024]{1,0:T(8,128)(2,1)} %bitcast.20, bf16[512,1024]{1,0:T(8,128)(2,1)S(1)} %get-tuple-element.22.keep_ref), custom_call_target="tpu_custom_call" | custom-call | flops 1073741824 | bytes 4194304 | tf_op jit(solution)/shard_map/far_product/pallas_call | solution.py:267
  7.6 3.0 %collective-permute-start.4 = (bf16[512,1024]{1,0:T(8,128)(2,1)S(1)}, bf16[512,1024]{1,0:T(8,128)(2,1)S(1)}, u32[]{:S(2)}, u32[]{:S(2)}) collective-permute-start(bf16[512,1024]{1,0:T(8,128)(2,1)S(1)} %fusion.7.send_ref), channel_id=1, source_target_pairs={{0,2},{1,3},{2,0},{3,1},{4,6},{5,7},{6,4},{7,5},{8,10},{9,11},{10,... | collective-permute-start | bytes 3145736 | tf_op jit(solution)/shard_map/ppermute | solution.py:313
  10.6 8.2 %near.1 = (f32[5,128,128]{2,1,0:T(8,128)S(1)}, f32[5,128,128]{2,1,0:T(8,128)S(1)}, f32[5,128,128]{2,1,0:T(8,128)S(1)}, f32[5,128,128]{2,1,0:T(8,128)S(1)}) custom-call(bf16[4096,1024]{1,0:T(8,128)(2,1)} %bitcast.18, bf16[4096,1024]{1,0:T(8,128)(2,1)} %bitcast.21, bf16[512,1024]{1,0:T(8,128)(2,1)S(1)} %get-tuple-element.22.keep_ref, ...), custom_call_target="tpu_custom_call" | custom-call | flops 4831838208 | bytes 9437184 | tf_op jit(solution)/shard_map/near/pallas_call | solution.py:231
  18.9 0.5 collective-permute-start.1
  19.4 2.7 %far_product.3.both_ref = bf16[1024,512]{1,0:T(8,128)(2,1)S(1)} custom-call(bf16[4096,1024]{1,0:T(8,128)(2,1)} %bitcast.19, bf16[4096,1024]{1,0:T(8,128)(2,1)} %bitcast.22, bf16[512,1024]{1,0:T(8,128)(2,1)S(1)} %get-tuple-element.22.keep_ref, bf16[1024,512]{1,0:T(8,128)(2,1)S(1)} %collective-permute-done.5.refs_0_), custom_call_target="tpu_custom_call" | custom-call | flops 1073741824 | bytes 4194304 | tf_op jit(solution)/shard_map/far_product/pallas_call | solution.py:267
  22.2 11.8 %collective-permute-done.4.sel_ref = bf16[512,1024]{1,0:T(8,128)(2,1)S(1)} collective-permute-done((bf16[512,1024]{1,0:T(8,128)(2,1)S(1)}, bf16[512,1024]{1,0:T(8,128)(2,1)S(1)}, u32[]{:S(2)}, u32[]{:S(2)}) %collective-permute-start.4) | collective-permute-done | bytes 1048608 | tf_op jit(solution)/shard_map/ppermute | solution.py:313
  34.0 0.9 far.1
  35.1 1.8 %collective-permute-start.3 = (f32[5,128,128]{2,1,0:T(8,128)S(1)}, f32[5,128,128]{2,1,0:T(8,128)S(1)}, u32[]{:S(2)}, u32[]{:S(2)}) collective-permute-start(f32[5,128,128]{2,1,0:T(8,128)S(1)} %add.27), channel_id=1, source_target_pairs={{0,2},{1,3},{2,0},{3,1},{4,6},{5,7},{6,4},{7,5},{8,10},{9,11},{10,... | collective-permute-start | bytes 983048 | tf_op jit(solution)/shard_map/ppermute | solution.py:320
  36.9 8.4 %collective-permute-done.3 = f32[5,128,128]{2,1,0:T(8,128)S(1)} collective-permute-done((f32[5,128,128]{2,1,0:T(8,128)S(1)}, f32[5,128,128]{2,1,0:T(8,128)S(1)}, u32[]{:S(2)}, u32[]{:S(2)}) %collective-permute-start.3) | collective-permute-done | bytes 327712 | tf_op jit(solution)/shard_map/ppermute | solution.py:320
  45.3 1.8 %collective-permute-start.7 = (f32[5,128,128]{2,1,0:T(8,128)S(1)}, f32[5,128,128]{2,1,0:T(8,128)S(1)}, u32[]{:S(2)}, u32[]{:S(2)}) collective-permute-start(f32[5,128,128]{2,1,0:T(8,128)S(1)} %add_add_fusion), channel_id=1, source_target_pairs={{0,2},{1,3},{2,0},{3,1},{4,6},{5,7},{6,4},{7,5},{8,10},{9,11},{10,... | collective-permute-start | bytes 983048 | tf_op jit(solution)/shard_map/ppermute | solution.py:336
  47.2 7.5 %collective-permute-done.7 = f32[5,128,128]{2,1,0:T(8,128)S(1)} collective-permute-done((f32[5,128,128]{2,1,0:T(8,128)S(1)}, f32[5,128,128]{2,1,0:T(8,128)S(1)}, u32[]{:S(2)}, u32[]{:S(2)}) %collective-permute-start.7) | collective-permute-done | bytes 327712 | tf_op jit(solution)/shard_map/ppermute | solution.py:336
  54.8 0.6 iota_reduce_fusion
  55.4 1.0 collective-permute-done.8.theirs_ref
  56.4 13.3 %factor.1 = f32[128,512]{1,0:T(8,128)} custom-call(s32[8]{0:T(128)S(1)} %copy-done.1, f32[5,128,128]{2,1,0:T(8,128)S(1)} %mul.3.mine_ref, f32[5,128,128]{2,1,0:T(8,128)S(1)} %collective-permute-done.8.theirs_ref), custom_call_target="tpu_custom_call" | custom-call | tf_op jit(solution)/shard_map/factor/pallas_call | solution.py:338
  69.7 6.0 %all-to-all-start = ((f32[8,16,512]{2,1,0:T(8,128)}), f32[8,16,512]{2,1,0:T(8,128)S(1)}, u32[]{:S(2)}, u32[]{:S(2)}) async-start(f32[8,16,512]{2,1,0:T(8,128)} %bitcast.5), calls=%async_computation | async-start | bytes 524288 | tf_op jit(solution)/shard_map/all_to_all | solution.py:295
  75.8 9.2 %all-to-all-done = f32[8,16,512]{2,1,0:T(8,128)S(1)} async-done(((f32[8,16,512]{2,1,0:T(8,128)}), f32[8,16,512]{2,1,0:T(8,128)S(1)}, u32[]{:S(2)}, u32[]{:S(2)}) %all-to-all-start) | async-done | bytes 262176 | tf_op jit(solution)/shard_map/all_to_all | solution.py:295
  85.0 0.6 gather_fusion
  85.6 12.0 %all_to_all.10 = f32[8,16,512]{2,1,0:T(8,128)S(1)} all-to-all(f32[8,16,512]{2,1,0:T(8,128)S(1)} %broadcast_select_fusion.1), channel_id=1, replica_groups=mesh['blk'=8,'slab'=4] {'blk'}, dimensions={0} | all-to-all | bytes 524288 | tf_op jit(solution)/shard_map/all_to_all | solution.py:297
  97.6 0.7 copy.8
  (21 shorter events, 0.6 us)
Async XLA Ops:
  0.0 1.6 %copy-start = (bf16[1,1024,1024]{2,1,0:T(8,128)(2,1)S(1)}, bf16[1,1024,1024]{2,1,0:T(8,128)(2,1)}, u32[]{:S(2)}) copy-start(bf16[1,1024,1024]{2,1,0:T(8,128)(2,1)} %param.8) | copy-start | bytes 6291460
  4.2 6.4 %collective-permute-start = (bf16[512,1024]{1,0:T(8,128)(2,1)S(1)}, bf16[512,1024]{1,0:T(8,128)(2,1)S(1)}, u32[]{:S(2)}, u32[]{:S(2)}) collective-permute-start(bf16[512,1024]{1,0:T(8,128)(2,1)S(1)} %get-tuple-element.21), channel_id=1, source_target_pairs={{0,1},{1,0},{2,3},{3,2},{4,5},{5,4},{6,7},{7,6},{8,9},{9,8},{10,11... | collective-permute-start | bytes 3145736 | tf_op jit(solution)/shard_map/ppermute | solution.py:315
  7.5 11.9 %collective-permute-start.5 = (bf16[1024,512]{1,0:T(8,128)(2,1)S(1)}, bf16[1024,512]{1,0:T(8,128)(2,1)S(1)}, u32[]{:S(2)}, u32[]{:S(2)}) collective-permute-start(bf16[1024,512]{1,0:T(8,128)(2,1)S(1)} %far_product.2), channel_id=1, source_target_pairs={{0,1},{1,0},{2,3},{3,2},{4,5},{5,4},{6,7},{7,6},{8,9},{9,8},{10,11... | collective-permute-start | bytes 3145736 | tf_op jit(solution)/shard_map/ppermute | solution.py:317
  7.6 26.4 %collective-permute-start.4 = (bf16[512,1024]{1,0:T(8,128)(2,1)S(1)}, bf16[512,1024]{1,0:T(8,128)(2,1)S(1)}, u32[]{:S(2)}, u32[]{:S(2)}) collective-permute-start(bf16[512,1024]{1,0:T(8,128)(2,1)S(1)} %fusion.7.send_ref), channel_id=1, source_target_pairs={{0,2},{1,3},{2,0},{3,1},{4,6},{5,7},{6,4},{7,5},{8,10},{9,11},{10,... | collective-permute-start | bytes 3145736 | tf_op jit(solution)/shard_map/ppermute | solution.py:313
  18.9 16.2 %collective-permute-start.2 = (f32[5,128,128]{2,1,0:T(8,128)S(1)}, f32[5,128,128]{2,1,0:T(8,128)S(1)}, u32[]{:S(2)}, u32[]{:S(2)}) collective-permute-start(f32[5,128,128]{2,1,0:T(8,128)S(1)} %get-tuple-element.16), channel_id=1, source_target_pairs={{0,1},{1,0},{2,3},{3,2},{4,5},{5,4},{6,7},{7,6},{8,9},{9,8},{10,11... | collective-permute-start | bytes 983048 | tf_op jit(solution)/shard_map/ppermute | solution.py:319
  18.9 18.0 %collective-permute-start.1 = (f32[5,128,128]{2,1,0:T(8,128)S(1)}, f32[5,128,128]{2,1,0:T(8,128)S(1)}, u32[]{:S(2)}, u32[]{:S(2)}) collective-permute-start(f32[5,128,128]{2,1,0:T(8,128)S(1)} %get-tuple-element.14), channel_id=1, source_target_pairs={{0,1},{1,0},{2,3},{3,2},{4,5},{5,4},{6,7},{7,6},{8,9},{9,8},{10,11... | collective-permute-start | bytes 983048 | tf_op jit(solution)/shard_map/ppermute | solution.py:322
  34.9 19.8 %copy-start.2 = (s32[8]{0:T(128)S(1)}, s32[8]{0:T(128)}, u32[]{:S(2)}) copy-start(s32[8]{0:T(128)} %param.11) | copy-start | bytes 100
  35.0 21.4 %copy-start.1 = (s32[8]{0:T(128)S(1)}, s32[8]{0:T(128)}, u32[]{:S(2)}) copy-start(s32[8]{0:T(128)} %orders_ref.1) | copy-start | bytes 100
  35.0 1.9 %collective-permute-start.6 = (f32[5,128,128]{2,1,0:T(8,128)S(1)}, f32[5,128,128]{2,1,0:T(8,128)S(1)}, u32[]{:S(2)}, u32[]{:S(2)}) collective-permute-start(f32[5,128,128]{2,1,0:T(8,128)S(1)} %get-tuple-element.18), channel_id=1, source_target_pairs={{0,1},{1,0},{2,3},{3,2},{4,5},{5,4},{6,7},{7,6},{8,9},{9,8},{10,11... | collective-permute-start | bytes 983048 | tf_op jit(solution)/shard_map/ppermute | solution.py:335
  35.1 10.2 %collective-permute-start.3 = (f32[5,128,128]{2,1,0:T(8,128)S(1)}, f32[5,128,128]{2,1,0:T(8,128)S(1)}, u32[]{:S(2)}, u32[]{:S(2)}) collective-permute-start(f32[5,128,128]{2,1,0:T(8,128)S(1)} %add.27), channel_id=1, source_target_pairs={{0,2},{1,3},{2,0},{3,1},{4,6},{5,7},{6,4},{7,5},{8,10},{9,11},{10,... | collective-permute-start | bytes 983048 | tf_op jit(solution)/shard_map/ppermute | solution.py:320
  45.3 9.3 %collective-permute-start.7 = (f32[5,128,128]{2,1,0:T(8,128)S(1)}, f32[5,128,128]{2,1,0:T(8,128)S(1)}, u32[]{:S(2)}, u32[]{:S(2)}) collective-permute-start(f32[5,128,128]{2,1,0:T(8,128)S(1)} %add_add_fusion), channel_id=1, source_target_pairs={{0,2},{1,3},{2,0},{3,1},{4,6},{5,7},{6,4},{7,5},{8,10},{9,11},{10,... | collective-permute-start | bytes 983048 | tf_op jit(solution)/shard_map/ppermute | solution.py:336
  54.7 1.7 %collective-permute-start.8 = (f32[5,128,128]{2,1,0:T(8,128)S(1)}, f32[5,128,128]{2,1,0:T(8,128)S(1)}, u32[]{:S(2)}, u32[]{:S(2)}) collective-permute-start(f32[5,128,128]{2,1,0:T(8,128)S(1)} %mul.3.mine_ref), channel_id=1, source_target_pairs={{0,1},{1,0},{2,3},{3,2},{4,5},{5,4},{6,7},{7,6},{8,9},{9,8},{10,11... | collective-permute-start | bytes 983048 | tf_op jit(solution)/shard_map/ppermute | solution.py:337
  69.7 15.2 %all-to-all-start = ((f32[8,16,512]{2,1,0:T(8,128)}), f32[8,16,512]{2,1,0:T(8,128)S(1)}, u32[]{:S(2)}, u32[]{:S(2)}) async-start(f32[8,16,512]{2,1,0:T(8,128)} %bitcast.5), calls=%async_computation | async-start | bytes 524288 | tf_op jit(solution)/shard_map/all_to_all | solution.py:295

commit v3 on v2

--- a/solution.py
+++ b/solution.py
@@ -98,10 +98,11 @@
             a_ref[there, span] = a_ref[there, span] - dot_f32(done[:, :LANES], done, TN)[first:]
 
 
-def factor_all(a_ref):
+def factor_all(a_ref, done=0):
     size = a_ref.shape[0]
     for start in range(0, size, LANES):
-        factor_rows(a_ref, start, size - start)
+        if start >= done:
+            factor_rows(a_ref, start, size - start)
         for row in range(start + LANES, size, LANES):
             left = a_ref[start : start + LANES, row : row + LANES]
             right = a_ref[start : start + LANES, row:]
@@ -133,10 +134,44 @@
     return jnp.where((rows < order) & (cols < order), block, 0.0) + (rows == cols).astype(F32)
 
 
-def upper_blocks(size):
+def deal(size):
     count = size // LANES
-    blocks = [(i, k) for k in range(count) for i in range(k + 1)]
-    return blocks[: len(blocks) // 2], blocks[len(blocks) // 2 :]
+    items = [(i, k) for i in range(count) for k in range(i, count) if i < k or i % 2 == 0]
+    first = [item for item in items if item[0] == 0]
+    rest = [item for item in items if item[0] > 0]
+    middle, centre = len(first) // 2, len(rest) // 2
+    return (first[:middle], rest[:centre]), (first[middle:], rest[centre:])
+
+
+def triangle():
+    row = lax.broadcasted_iota(jnp.int32, (LANES, LANES), 0)
+    return row - lax.broadcasted_iota(jnp.int32, (LANES, LANES), 1)
+
+
+def packed_shape(hands):
+    return (len(hands[0][0]) + len(hands[0][1])) * LANES + MICRO, LANES
+
+
+def deal_out(total_ref, hands, core, mine_ref, give_ref):
+    def sym(i, k):
+        i, k = i * LANES, k * LANES
+        return total_ref[i : i + LANES, k : k + LANES] + total_ref[k : k + LANES, i : i + LANES].T
+
+    for turn in range(2):
+        @pl.when(core == turn)
+        def _():
+            for ref, hand in ((mine_ref, hands[turn]), (give_ref, hands[1 - turn])):
+                items = hand[0] + hand[1]
+                tail = len(items) * LANES
+                ref[tail:, :] = jnp.zeros((ref.shape[0] - tail, LANES), F32)
+                for t, (i, k) in enumerate(items):
+                    block = sym(i, k)
+                    if i == k:
+                        other = sym(i + 1, i + 1)
+                        diagonal = jnp.sum(jnp.where(triangle() == 0, other, 0.0), axis=0, keepdims=True)
+                        ref[tail + i // 2 : tail + i // 2 + 1, :] = diagonal
+                        block = jnp.where(triangle() >= 0, block, other)
+                    ref[t * LANES : t * LANES + LANES, :] = block
 
 
 def position():
@@ -144,17 +179,56 @@
     return slab // 2, slab % 2
 
 
-def factor_kernel(halves, orders_ref, mine_ref, theirs_ref, out_ref, a_ref):
+def place_blocks(a_ref, order, items, block_of, row_of, wanted):
+    for t, (i, k) in enumerate(items):
+        block = block_of(t)
+        parts = [((i, k), block)]
+        if i == k:
+            flipped = block.T
+            one = jnp.where(triangle() >= 0, block, flipped)
+            parts = [((i, i), one)]
+            if wanted(i + 1):
+                other = jnp.where(triangle() < 0, block, flipped)
+                other = jnp.where(triangle() == 0, row_of(i // 2), other)
+                parts.append(((i + 1, i + 1), other))
+        for (i, k), block in parts:
+            if wanted(i):
+                i, k = i * LANES, k * LANES
+                a_ref[i : i + LANES, k : k + LANES] = assemble(block, i, k, order)
+
+
+def factor_first_kernel(hands, orders_ref, mine_ref, theirs_ref, a_ref):
     _, core = position()
     order = orders_ref[lax.axis_index("blk")]
     for turn in range(2):
         @pl.when(core == turn)
         def _():
-            for ref, half in ((mine_ref, halves[turn]), (theirs_ref, halves[1 - turn])):
-                for t, (i, k) in enumerate(half):
-                    i, k = i * LANES, k * LANES
-                    a_ref[i : i + LANES, k : k + LANES] = assemble(ref[t], i, k, order)
-    factor_all(a_ref)
+            for ref, hand in ((mine_ref, hands[turn]), (theirs_ref, hands[1 - turn])):
+                block_of = lambda t: ref[t * LANES : t * LANES + LANES, :]
+                place_blocks(a_ref, order, hand[0], block_of, None, lambda i: i == 0)
+    factor_rows(a_ref, 0, a_ref.shape[1])
+
+
+def factor_rest_kernel(
+    hands, orders_ref, top_ref, mine_ref, theirs_ref, mine_rest_ref, theirs_rest_ref, out_ref, a_ref
+):
+    _, core = position()
+    order = orders_ref[lax.axis_index("blk")]
+    done = top_ref.shape[0]
+    a_ref[:done, :] = top_ref[...]
+    for turn in range(2):
+        @pl.when(core == turn)
+        def _():
+            for ref, rest_ref, hand in (
+                (mine_ref, mine_rest_ref, hands[turn]),
+                (theirs_ref, theirs_rest_ref, hands[1 - turn]),
+            ):
+                tail = len(hand[1]) * LANES
+                row_of = lambda e: rest_ref[tail + e : tail + e + 1, :]
+                for part, part_ref in ((hand[0], ref), (hand[1], rest_ref)):
+                    block_of = lambda t: part_ref[t * LANES : t * LANES + LANES, :]
+                    place_blocks(a_ref, order, part, block_of, row_of, lambda i: i > 0)
+    factor_all(a_ref, done)
     own_rows(a_ref, out_ref, lax.axis_index("slab") * out_ref.shape[0])
 
 
@@ -162,17 +236,6 @@
     a_ref[...] = s_ref[...]
     factor_all(a_ref)
     own_rows(a_ref, out_ref, lax.axis_index("slab") * out_ref.shape[0])
-
-
-def split_upper(total_ref, halves, core, mine_ref, give_ref):
-    for turn in range(2):
-        @pl.when(core == turn)
-        def _():
-            for ref, half in ((mine_ref, halves[turn]), (give_ref, halves[1 - turn])):
-                for t, (i, k) in enumerate(half):
-                    i, k = i * LANES, k * LANES
-                    mirror = total_ref[k : k + LANES, i : i + LANES].T
-                    ref[t] = total_ref[i : i + LANES, k : k + LANES] + mirror
 
 
 def fetch(z_refs, use_x, slab, held_ref, sems, first):
@@ -190,7 +253,7 @@
 
 
 def near_kernel(
-    halves, x_ref, y_ref, keep_ref, send_ref, cross_ref,
+    hands, x_ref, y_ref, keep_ref, send_ref, cross_ref,
     side_mine_ref, side_give_ref, main_mine_ref, main_give_ref, main_ref, side_ref, held_ref, sems,
 ):
     chip, core = position()
@@ -217,19 +280,19 @@
         else:
             pl.when(core == 0)(functools.partial(add, t, keep_ref, cross_ref, 1.0, main_ref, False))
             pl.when(core == 1)(functools.partial(add, t, send_ref, cross_ref, 1.0, side_ref, False))
-    split_upper(side_ref, halves, core, side_mine_ref, side_give_ref)
-    split_upper(main_ref, halves, core, main_mine_ref, main_give_ref)
+    deal_out(side_ref, hands, core, side_mine_ref, side_give_ref)
+    deal_out(main_ref, hands, core, main_mine_ref, main_give_ref)
 
 
 def in_hbm(z):
     return pltpu.with_memory_space_constraint(z, pltpu.HBM)
 
 
-def near(halves, x, y, keep, send, cross):
+def near(hands, x, y, keep, send, cross):
     size, depth = keep.shape
-    blocks = (len(halves[0]), LANES, LANES)
+    blocks = packed_shape(hands)
     return pl.pallas_call(
-        functools.partial(near_kernel, halves),
+        functools.partial(near_kernel, hands),
         out_shape=(jax.ShapeDtypeStruct(blocks, F32),) * 4,
         in_specs=[ANY, ANY, VMEM, VMEM, VMEM],
         out_specs=(VMEM,) * 4,
@@ -278,10 +341,10 @@
     )(in_hbm(x), in_hbm(y), keep, *got)
 
 
-def far_kernel(halves, sel_ref, both_ref, mine_ref, give_ref, total_ref):
+def far_kernel(hands, sel_ref, both_ref, mine_ref, give_ref, total_ref):
     _, core = position()
     total_ref[...] = jnp.dot(sel_ref[...], both_ref[...], preferred_element_type=F32)
-    split_upper(total_ref, halves, core, mine_ref, give_ref)
+    deal_out(total_ref, hands, core, mine_ref, give_ref)
 
 
 def select_columns(v, index):
@@ -301,11 +364,11 @@
 def two_chips(x, y, v, index, orders, dest):
     slabs, groups = lax.axis_size("slab"), lax.axis_size("blk")
     depth, size = v.shape[0], index.shape[1]
-    halves = upper_blocks(size)
-    half = len(halves[0])
+    hands = deal(size)
+    top = len(hands[0][0]) * LANES
     to_core = [(s, s ^ 1) for s in range(slabs)]
     to_chip = [(s, s ^ 2) for s in range(slabs)]
-    blocks = jax.ShapeDtypeStruct((half, LANES, LANES), F32)
+    blocks = jax.ShapeDtypeStruct(packed_shape(hands), F32)
     chip, core = position()
     first, second = index
 
@@ -315,13 +378,13 @@
     cross = lax.ppermute(jnp.where(core == 0, send, keep), "slab", to_core)
     give = far_product(x, y, keep)
     got = lax.ppermute(give, "slab", to_core)
-    side_mine, side_give, main_mine, main_give = near(halves, x, y, keep, send, cross)
+    side_mine, side_give, main_mine, main_give = near(hands, x, y, keep, send, cross)
     side_sum = side_mine + lax.ppermute(side_give, "slab", to_core)
     early = lax.ppermute(side_sum, "slab", to_chip)
     both = far_product(x, y, keep, got)
     main_sum = main_mine + lax.ppermute(main_give, "slab", to_core)
     far_mine, far_give = pl.pallas_call(
-        functools.partial(far_kernel, halves),
+        functools.partial(far_kernel, hands),
         out_shape=(blocks, blocks),
         in_specs=[VMEM] * 2,
         out_specs=(VMEM, VMEM),
@@ -333,17 +396,32 @@
         compiler_params=pltpu.CompilerParams(vmem_limit_bytes=8 << 20),
     )(far, both)
     total = main_sum + early + (far_mine + lax.ppermute(far_give, "slab", to_core))
-    schur = total * lax.ppermute(total, "slab", to_chip)
+    first_got = lax.ppermute(total[:top], "slab", to_chip)
+    rest_got = lax.ppermute(total[top:], "slab", to_chip)
+    schur = total[:top] * first_got
     other = lax.ppermute(schur, "slab", to_core)
-    own = pl.pallas_call(
-        functools.partial(factor_kernel, halves),
-        out_shape=jax.ShapeDtypeStruct((size // slabs, size), F32),
+    upper = pl.pallas_call(
+        functools.partial(factor_first_kernel, hands),
+        out_shape=jax.ShapeDtypeStruct((LANES, size), F32),
         in_specs=[SMEM, VMEM, VMEM],
         out_specs=VMEM,
-        scratch_shapes=[pltpu.VMEM((size, size), F32)],
-        name="factor",
+        cost_estimate=pl.CostEstimate(
+            flops=LANES * LANES * size, bytes_accessed=16 * LANES * size, transcendentals=LANES
+        ),
+        name="factor_first",
         compiler_params=pltpu.CompilerParams(vmem_limit_bytes=8 << 20),
     )(orders, schur, other)
+    schur_rest = total[top:] * rest_got
+    other_rest = lax.ppermute(schur_rest, "slab", to_core)
+    own = pl.pallas_call(
+        functools.partial(factor_rest_kernel, hands),
+        out_shape=jax.ShapeDtypeStruct((size // slabs, size), F32),
+        in_specs=[SMEM] + [VMEM] * 5,
+        out_specs=VMEM,
+        scratch_shapes=[pltpu.VMEM((size, size), F32)],
+        name="factor_rest",
+        compiler_params=pltpu.CompilerParams(vmem_limit_bytes=8 << 20),
+    )(orders, upper, schur, other, schur_rest, other_rest)
     return place(own, dest, groups)
 
 

time: 98.6 us -> 96.9 us (0.983)
  waiting for transfers between devices: 37.9 us -> 34.2 us
  Pallas kernels: 27.9 us -> 28.9 us
    ppermute x1 -> x3, waiting for transfers between devices: 7.5 us -> 5.73 us  [the longest x1 4.2 us: two_chips(): first_got = lax.ppermute(total[:top], 'slab', to_chip)]
    ppermute x1, waiting for transfers between devices: 8.35 us -> 7.04 us  [two_chips(): early = lax.ppermute(side_sum, 'slab', to_chip)]
    pallas_call x3 -> x4, Pallas kernels: 22.5 us -> 23.5 us  [the longest x1 10.5 us: two_chips(): pl.pallas_call(functools.partial(factor_rest_kernel, hands), out_shape=ja...]
    ppermute x1 -> x3, starting transfers between devices: 1.81 us -> 2.23 us  [the longest x1 1.81 us: two_chips(): first_got = lax.ppermute(total[:top], 'slab', to_chip)]
  transfers between devices with their start and end apart: 10 -> 12, of which waited for: 5 -> 5; matrix products, arithmetic and copies ran while one was open for 1% -> 1% of each run, Pallas kernels for 15% -> 19%
where the time goes in v3:
time: 96.9 us; the launch traced here: 96.6 us
  waiting for transfers between devices  34.2 us (35%)
  Pallas kernels  28.9 us (30%)
  starting transfers between devices  14.4 us (15%)
  blocking collectives  12.5 us (13%)
  matrix products  2.58 us (3%)
  local copies, waits for them, and re-layouts  2.06 us (2%)
  other arithmetic  1.76 us (2%)
    all_to_all x1, blocking collectives, place(): pieces = lax.all_to_all(pieces, 'blk', 0, 0)  12.5 us
    ppermute x1, waiting for transfers between devices, two_chips(): far = lax.ppermute(send, 'slab', to_chip)  11.8 us
    pallas_call x1, Pallas kernels, two_chips(): pl.pallas_call(functools.partial(factor_rest_kernel, hands), out_shape=ja...  10.5 us
    all_to_all x1, waiting for transfers between devices, place(): pieces = lax.all_to_all(pieces, 'blk', 0, 0)  9.54 us
    pallas_call x1, Pallas kernels, near(): pl.pallas_call(functools.partial(near_kernel, hands), out_shape=(jax.Shap...  8.23 us
    ppermute x1, waiting for transfers between devices, two_chips(): early = lax.ppermute(side_sum, 'slab', to_chip)  7.04 us
    all_to_all x1, starting transfers between devices, place(): pieces = lax.all_to_all(pieces, 'blk', 0, 0)  6.03 us
    pallas_call x2, Pallas kernels, far_product(): pl.pallas_call(far_product_kernel, out_shape=jax.ShapeDtypeStruct((depth,...  5.46 us
  transfers between devices with their start and end apart: 12, of which 5 were waited for; matrix products, arithmetic and copies ran while one was open for 1% of the time, Pallas kernels for 19%

profile of v3, /device:TPU:0, one launch (start us, length us, event | category | flops | bytes accessed | tf_op | source)
XLA Modules:
  0.0 96.6 jit_solution(12684909958653717641)
XLA Ops:
  0.0 0.9 broadcast_select_fusion.3
  0.9 0.8 copy-done
  1.6 1.3 %fusion.7.send_ref = bf16[512,1024]{1,0:T(8,128)(2,1)S(1)} fusion(bf16[1,1024,1024]{2,1,0:T(8,128)(2,1)S(1)} %copy-done, s32[512]{0:T(512)S(1)} %bitcast.25), kind=kOutput, calls=%fused_computation.8 | convolution fusion | flops 1074790400 | bytes 3147776 | tf_op jit(solution)/shard_map/dot_general | solution.py:352
  2.9 1.3 %broadcast_select_fusion = (bf16[512,1024]{1,0:T(8,128)(2,1)S(1)}, bf16[512,1024]{1,0:T(8,128)(2,1)S(1)}) fusion(bf16[512,1024]{1,0:T(8,128)(2,1)S(1)} %fusion.7.send_ref, pred[]{:T(512)S(6)} %eq.48, bf16[1,1024,1024]{2,1,0:T(8,128)(2,1)S(1)} %copy-done, s32[512]{0:T(512)S(1)} %bitcast.24), kind=kOutput, calls=%fused_computation.11 | convolution fusion | flops 1075314688 | bytes 5244929 | tf_op jit(solution)/shard_map/dot_general | solution.py:352
  4.2 0.6 collective-permute-start
  4.8 2.7 %far_product.2 = bf16[1024,512]{1,0:T(8,128)(2,1)S(1)} custom-call(bf16[4096,1024]{1,0:T(8,128)(2,1)} %bitcast.17, bf16[4096,1024]{1,0:T(8,128)(2,1)} %bitcast.20, bf16[512,1024]{1,0:T(8,128)(2,1)S(1)} %get-tuple-element.22.keep_ref), custom_call_target="tpu_custom_call" | custom-call | flops 1073741824 | bytes 4194304 | tf_op jit(solution)/shard_map/far_product/pallas_call | solution.py:330
  7.6 3.0 %collective-permute-start.4 = (bf16[512,1024]{1,0:T(8,128)(2,1)S(1)}, bf16[512,1024]{1,0:T(8,128)(2,1)S(1)}, u32[]{:S(2)}, u32[]{:S(2)}) collective-permute-start(bf16[512,1024]{1,0:T(8,128)(2,1)S(1)} %fusion.7.send_ref), channel_id=1, source_target_pairs={{0,2},{1,3},{2,0},{3,1},{4,6},{5,7},{6,4},{7,5},{8,10},{9,11},{10,... | collective-permute-start | bytes 3145736 | tf_op jit(solution)/shard_map/ppermute | solution.py:376
  10.6 8.2 %near.1 = (f32[520,128]{1,0:T(8,128)S(1)}, f32[520,128]{1,0:T(8,128)S(1)}, f32[520,128]{1,0:T(8,128)S(1)}, f32[520,128]{1,0:T(8,128)S(1)}) custom-call(bf16[4096,1024]{1,0:T(8,128)(2,1)} %bitcast.18, bf16[4096,1024]{1,0:T(8,128)(2,1)} %bitcast.21, bf16[512,1024]{1,0:T(8,128)(2,1)S(1)} %get-tuple-element.22.keep_ref, bf16[512,1024]{1,0:T(8,128)(2,1)S(1)} %fusion.7.send_ref, ...), custom_call_target="tpu_custom_call" | custom-call | flops 4831838208 | bytes 9437184 | tf_op jit(solution)/shard_map/near/pallas_call | solution.py:294
  19.4 2.7 %far_product.3.both_ref = bf16[1024,512]{1,0:T(8,128)(2,1)S(1)} custom-call(bf16[4096,1024]{1,0:T(8,128)(2,1)} %bitcast.19, bf16[4096,1024]{1,0:T(8,128)(2,1)} %bitcast.22, bf16[512,1024]{1,0:T(8,128)(2,1)S(1)} %get-tuple-element.22.keep_ref, bf16[1024,512]{1,0:T(8,128)(2,1)S(1)} %collective-permute-done.5.refs_0_), custom_call_target="tpu_custom_call" | custom-call | flops 1073741824 | bytes 4194304 | tf_op jit(solution)/shard_map/far_product/pallas_call | solution.py:330
  22.2 11.8 %collective-permute-done.4.sel_ref = bf16[512,1024]{1,0:T(8,128)(2,1)S(1)} collective-permute-done((bf16[512,1024]{1,0:T(8,128)(2,1)S(1)}, bf16[512,1024]{1,0:T(8,128)(2,1)S(1)}, u32[]{:S(2)}, u32[]{:S(2)}) %collective-permute-start.4) | collective-permute-done | bytes 1048608 | tf_op jit(solution)/shard_map/ppermute | solution.py:376
  34.0 0.9 far.1
  35.1 1.8 %collective-permute-start.3 = (f32[520,128]{1,0:T(8,128)S(1)}, f32[520,128]{1,0:T(8,128)S(1)}, u32[]{:S(2)}, u32[]{:S(2)}) collective-permute-start(f32[520,128]{1,0:T(8,128)S(1)} %add.27), channel_id=1, source_target_pairs={{0,2},{1,3},{2,0},{3,1},{4,6},{5,7},{6,4},{7,5},{8,10},{9,11},{10,... | collective-permute-start | bytes 798728 | tf_op jit(solution)/shard_map/ppermute | solution.py:383
  36.9 7.0 %collective-permute-done.3 = f32[520,128]{1,0:T(8,128)S(1)} collective-permute-done((f32[520,128]{1,0:T(8,128)S(1)}, f32[520,128]{1,0:T(8,128)S(1)}, u32[]{:S(2)}, u32[]{:S(2)}) %collective-permute-start.3) | collective-permute-done | bytes 266272 | tf_op jit(solution)/shard_map/ppermute | solution.py:383
  44.1 1.8 %collective-permute-start.7 = (f32[256,128]{1,0:T(8,128)S(1)}, f32[256,128]{1,0:T(8,128)S(1)}, u32[]{:S(2)}, u32[]{:S(2)}) collective-permute-start(f32[256,128]{1,0:T(8,128)S(1)} %slice.14), channel_id=1, source_target_pairs={{0,2},{1,3},{2,0},{3,1},{4,6},{5,7},{6,4},{7,5},{8,10},{9,11},{10,... | collective-permute-start | bytes 393224 | tf_op jit(solution)/shard_map/ppermute | solution.py:399
  46.3 4.2 %collective-permute-done.7 = f32[256,128]{1,0:T(8,128)S(1)} collective-permute-done((f32[256,128]{1,0:T(8,128)S(1)}, f32[256,128]{1,0:T(8,128)S(1)}, u32[]{:S(2)}, u32[]{:S(2)}) %collective-permute-start.7) | collective-permute-done | bytes 131104 | tf_op jit(solution)/shard_map/ppermute | solution.py:399
  50.6 1.5 %collective-permute-done.9 = f32[264,128]{1,0:T(8,128)S(1)} collective-permute-done((f32[264,128]{1,0:T(8,128)S(1)}, f32[264,128]{1,0:T(8,128)S(1)}, u32[]{:S(2)}, u32[]{:S(2)}) %collective-permute-start.9) | collective-permute-done | bytes 135200 | tf_op jit(solution)/shard_map/ppermute | solution.py:400
  52.2 0.6 iota_reduce_fusion
  52.8 3.8 %factor_first.1.top_ref = f32[128,512]{1,0:T(8,128)S(1)} custom-call(s32[8]{0:T(128)S(1)} %copy-done.1, f32[256,128]{1,0:T(8,128)S(1)} %slice_multiply_fusion.mine_ref, f32[256,128]{1,0:T(8,128)S(1)} %collective-permute-done.8.theirs_ref), custom_call_target="tpu_custom_call" | custom-call | flops 8388608 | bytes 1048576 | tf_op jit(solution)/shard_map/factor_first/pallas_call | solution.py:403
  56.7 10.5 %factor_rest.1 = f32[128,512]{1,0:T(8,128)} custom-call(s32[8]{0:T(128)S(1)} %copy-done.1, f32[128,512]{1,0:T(8,128)S(1)} %factor_first.1.top_ref, f32[256,128]{1,0:T(8,128)S(1)} %slice_multiply_fusion.mine_ref, f32[256,128]{1,0:T(8,128)S(1)} %collective-permute-done.8.theirs_ref, f32[264,128]{1,0:T(8,128)S(1)} %slice_multiply_fusion.1.mine_rest_ref, ...), custom_call_target="tpu_custom_call" | custom-call | tf_op jit(solution)/shard_map/factor_rest/pallas_call | solution.py:416
  67.1 6.0 %all-to-all-start = ((f32[8,16,512]{2,1,0:T(8,128)}), f32[8,16,512]{2,1,0:T(8,128)S(1)}, u32[]{:S(2)}, u32[]{:S(2)}) async-start(f32[8,16,512]{2,1,0:T(8,128)} %bitcast.5), calls=%async_computation | async-start | bytes 524288 | tf_op jit(solution)/shard_map/all_to_all | solution.py:358
  73.2 9.5 %all-to-all-done = f32[8,16,512]{2,1,0:T(8,128)S(1)} async-done(((f32[8,16,512]{2,1,0:T(8,128)}), f32[8,16,512]{2,1,0:T(8,128)S(1)}, u32[]{:S(2)}, u32[]{:S(2)}) %all-to-all-start) | async-done | bytes 262176 | tf_op jit(solution)/shard_map/all_to_all | solution.py:358
  82.7 0.6 gather_fusion
  83.4 12.5 %all_to_all.10 = f32[8,16,512]{2,1,0:T(8,128)S(1)} all-to-all(f32[8,16,512]{2,1,0:T(8,128)S(1)} %broadcast_select_fusion.1), channel_id=1, replica_groups=mesh['blk'=8,'slab'=4] {'blk'}, dimensions={0} | all-to-all | bytes 524288 | tf_op jit(solution)/shard_map/all_to_all | solution.py:360
  95.9 0.7 copy.8
  (29 shorter events, 1.6 us)
Async XLA Ops:
  0.0 1.6 %copy-start = (bf16[1,1024,1024]{2,1,0:T(8,128)(2,1)S(1)}, bf16[1,1024,1024]{2,1,0:T(8,128)(2,1)}, u32[]{:S(2)}) copy-start(bf16[1,1024,1024]{2,1,0:T(8,128)(2,1)} %param.8) | copy-start | bytes 6291460
  4.2 6.4 %collective-permute-start = (bf16[512,1024]{1,0:T(8,128)(2,1)S(1)}, bf16[512,1024]{1,0:T(8,128)(2,1)S(1)}, u32[]{:S(2)}, u32[]{:S(2)}) collective-permute-start(bf16[512,1024]{1,0:T(8,128)(2,1)S(1)} %get-tuple-element.21), channel_id=1, source_target_pairs={{0,1},{1,0},{2,3},{3,2},{4,5},{5,4},{6,7},{7,6},{8,9},{9,8},{10,11... | collective-permute-start | bytes 3145736 | tf_op jit(solution)/shard_map/ppermute | solution.py:378
  7.5 11.9 %collective-permute-start.5 = (bf16[1024,512]{1,0:T(8,128)(2,1)S(1)}, bf16[1024,512]{1,0:T(8,128)(2,1)S(1)}, u32[]{:S(2)}, u32[]{:S(2)}) collective-permute-start(bf16[1024,512]{1,0:T(8,128)(2,1)S(1)} %far_product.2), channel_id=1, source_target_pairs={{0,1},{1,0},{2,3},{3,2},{4,5},{5,4},{6,7},{7,6},{8,9},{9,8},{10,11... | collective-permute-start | bytes 3145736 | tf_op jit(solution)/shard_map/ppermute | solution.py:380
  7.6 26.4 %collective-permute-start.4 = (bf16[512,1024]{1,0:T(8,128)(2,1)S(1)}, bf16[512,1024]{1,0:T(8,128)(2,1)S(1)}, u32[]{:S(2)}, u32[]{:S(2)}) collective-permute-start(bf16[512,1024]{1,0:T(8,128)(2,1)S(1)} %fusion.7.send_ref), channel_id=1, source_target_pairs={{0,2},{1,3},{2,0},{3,1},{4,6},{5,7},{6,4},{7,5},{8,10},{9,11},{10,... | collective-permute-start | bytes 3145736 | tf_op jit(solution)/shard_map/ppermute | solution.py:376
  18.9 16.2 %collective-permute-start.2 = (f32[520,128]{1,0:T(8,128)S(1)}, f32[520,128]{1,0:T(8,128)S(1)}, u32[]{:S(2)}, u32[]{:S(2)}) collective-permute-start(f32[520,128]{1,0:T(8,128)S(1)} %get-tuple-element.16), channel_id=1, source_target_pairs={{0,1},{1,0},{2,3},{3,2},{4,5},{5,4},{6,7},{7,6},{8,9},{9,8},{10,11... | collective-permute-start | bytes 798728 | tf_op jit(solution)/shard_map/ppermute | solution.py:382
  18.9 18.0 %collective-permute-start.1 = (f32[520,128]{1,0:T(8,128)S(1)}, f32[520,128]{1,0:T(8,128)S(1)}, u32[]{:S(2)}, u32[]{:S(2)}) collective-permute-start(f32[520,128]{1,0:T(8,128)S(1)} %get-tuple-element.14), channel_id=1, source_target_pairs={{0,1},{1,0},{2,3},{3,2},{4,5},{5,4},{6,7},{7,6},{8,9},{9,8},{10,11... | collective-permute-start | bytes 798728 | tf_op jit(solution)/shard_map/ppermute | solution.py:385
  35.0 17.2 %copy-start.2 = (s32[8]{0:T(128)S(1)}, s32[8]{0:T(128)}, u32[]{:S(2)}) copy-start(s32[8]{0:T(128)} %param.11) | copy-start | bytes 100
  35.0 17.8 %copy-start.1 = (s32[8]{0:T(128)S(1)}, s32[8]{0:T(128)}, u32[]{:S(2)}) copy-start(s32[8]{0:T(128)} %orders_ref.3) | copy-start | bytes 100
  35.0 1.9 %collective-permute-start.6 = (f32[520,128]{1,0:T(8,128)S(1)}, f32[520,128]{1,0:T(8,128)S(1)}, u32[]{:S(2)}, u32[]{:S(2)}) collective-permute-start(f32[520,128]{1,0:T(8,128)S(1)} %get-tuple-element.18), channel_id=1, source_target_pairs={{0,1},{1,0},{2,3},{3,2},{4,5},{5,4},{6,7},{7,6},{8,9},{9,8},{10,11... | collective-permute-start | bytes 798728 | tf_op jit(solution)/shard_map/ppermute | solution.py:398
  35.1 8.9 %collective-permute-start.3 = (f32[520,128]{1,0:T(8,128)S(1)}, f32[520,128]{1,0:T(8,128)S(1)}, u32[]{:S(2)}, u32[]{:S(2)}) collective-permute-start(f32[520,128]{1,0:T(8,128)S(1)} %add.27), channel_id=1, source_target_pairs={{0,2},{1,3},{2,0},{3,1},{4,6},{5,7},{6,4},{7,5},{8,10},{9,11},{10,... | collective-permute-start | bytes 798728 | tf_op jit(solution)/shard_map/ppermute | solution.py:383
  44.1 6.4 %collective-permute-start.7 = (f32[256,128]{1,0:T(8,128)S(1)}, f32[256,128]{1,0:T(8,128)S(1)}, u32[]{:S(2)}, u32[]{:S(2)}) collective-permute-start(f32[256,128]{1,0:T(8,128)S(1)} %slice.14), channel_id=1, source_target_pairs={{0,2},{1,3},{2,0},{3,1},{4,6},{5,7},{6,4},{7,5},{8,10},{9,11},{10,... | collective-permute-start | bytes 393224 | tf_op jit(solution)/shard_map/ppermute | solution.py:399
  45.9 6.2 %collective-permute-start.9 = (f32[264,128]{1,0:T(8,128)S(1)}, f32[264,128]{1,0:T(8,128)S(1)}, u32[]{:S(2)}, u32[]{:S(2)}) collective-permute-start(f32[264,128]{1,0:T(8,128)S(1)} %slice.15), channel_id=1, source_target_pairs={{0,2},{1,3},{2,0},{3,1},{4,6},{5,7},{6,4},{7,5},{8,10},{9,11},{10,... | collective-permute-start | bytes 405512 | tf_op jit(solution)/shard_map/ppermute | solution.py:400
  50.5 2.4 %collective-permute-start.8 = (f32[256,128]{1,0:T(8,128)S(1)}, f32[256,128]{1,0:T(8,128)S(1)}, u32[]{:S(2)}, u32[]{:S(2)}) collective-permute-start(f32[256,128]{1,0:T(8,128)S(1)} %slice_multiply_fusion.mine_ref), channel_id=1, source_target_pairs={{0,1},{1,0},{2,3},{3,2},{4,5},{5,4},{6,7},{7,6},{8,9},{9,8},{10,11... | collective-permute-start | bytes 393224 | tf_op jit(solution)/shard_map/ppermute | solution.py:402
  52.1 4.5 %collective-permute-start.10 = (f32[264,128]{1,0:T(8,128)S(1)}, f32[264,128]{1,0:T(8,128)S(1)}, u32[]{:S(2)}, u32[]{:S(2)}) collective-permute-start(f32[264,128]{1,0:T(8,128)S(1)} %slice_multiply_fusion.1.mine_rest_ref), channel_id=1, source_target_pairs={{0,1},{1,0},{2,3},{3,2},{4,5},{5,4},{6,7},{7,6},{8,9},{9,8},{10,11... | collective-permute-start | bytes 405512 | tf_op jit(solution)/shard_map/ppermute | solution.py:415
  67.1 15.6 %all-to-all-start = ((f32[8,16,512]{2,1,0:T(8,128)}), f32[8,16,512]{2,1,0:T(8,128)S(1)}, u32[]{:S(2)}, u32[]{:S(2)}) async-start(f32[8,16,512]{2,1,0:T(8,128)} %bitcast.5), calls=%async_computation | async-start | bytes 524288 | tf_op jit(solution)/shard_map/all_to_all | solution.py:358

commit v4 on v3

--- a/solution.py
+++ b/solution.py
@@ -12,8 +12,7 @@
 BF16 = jnp.bfloat16
 LANES = 128
 MICRO = 8
-GROUP = 4
-AHEAD = 1
+GROUP = 8
 VMEM = pl.BlockSpec(memory_space=pltpu.VMEM)
 SMEM = pl.BlockSpec(memory_space=pltpu.SMEM)
 ANY = pl.BlockSpec(memory_space=pl.ANY)
@@ -61,20 +60,27 @@
             for j in range(k + 1, MICRO):
                 for i in range(j, MICRO):
                     low[i, j] = low[i, j] - low[i, k] * low[j, k]
-        wide = [row_splat(rows, i) for i in range(MICRO)]
+        sub = lax.broadcasted_iota(jnp.int32, (MICRO, LANES), 0)
+        wide = []
+        left = rows
         for k in range(MICRO):
-            wide[k] = by_tile(lambda x: x * inv[k], wide[k])
-            for i in range(k + 1, MICRO):
-                wide[i] = by_tile(lambda x, u: x - low[i, k] * u, wide[i], wide[k])
-        sub = lax.broadcasted_iota(jnp.int32, (MICRO, width), 0)
-        lane = lax.broadcasted_iota(jnp.int32, (MICRO, width), 1)
-        packed = wide[0]
+            u = by_tile(lambda x: x * inv[k], row_splat(left, k))
+            wide.append(u)
+            if k + 1 < MICRO:
+                column = jnp.where(sub == k + 1, low[k + 1, k], 0.0)
+                for i in range(k + 2, MICRO):
+                    column = jnp.where(sub == i, low[i, k], column)
+                left = by_tile(lambda x, y: x - column * y, left, u)
+        scale = inv[0]
         for k in range(1, MICRO):
-            packed = jnp.where(sub == k, wide[k], packed)
-        a_ref[here, span] = jnp.where(lane >= sub + base, packed, 0.0)
+            scale = jnp.where(sub == k, inv[k], scale)
+        upper = lax.broadcasted_iota(jnp.int32, (MICRO, LANES), 1) >= sub + base
+        a_ref[here, start : start + LANES] = jnp.where(upper, left[:, :LANES] * scale, 0.0)
+        for t in range(LANES, width, LANES):
+            a_ref[here, start + t : start + t + LANES] = left[:, t : t + LANES] * scale
         group_end = (m // GROUP + 1) * GROUP
         cols = None
-        for later in range(m + 1, min(group_end + AHEAD, count)):
+        for later in range(m + 1, min(group_end + 1, count)):
             there = slice(start + MICRO * later, start + MICRO * later + MICRO)
             rest = a_ref[there, span]
             head = rest[:, :LANES]
@@ -91,9 +97,9 @@
             for k in range(MICRO):
                 rest = by_tile(lambda x, u: x - part[k] * u, rest, wide[k])
             a_ref[there, span] = rest
-        if m + 1 == group_end and group_end + AHEAD < count:
+        if m + 1 == group_end and group_end + 1 < count:
             done = a_ref[start + MICRO * (group_end - GROUP) : start + MICRO * group_end, span]
-            first = MICRO * (group_end + AHEAD)
+            first = MICRO * (group_end + 1)
             there = slice(start + first, start + LANES)
             a_ref[there, span] = a_ref[there, span] - dot_f32(done[:, :LANES], done, TN)[first:]
 

time: 96.9 us -> 95.9 us (0.990)
  Pallas kernels: 28.9 us -> 27.9 us
where the time goes in v4:
time: 95.9 us; the launch traced here: 95.6 us
  waiting for transfers between devices  34.2 us (36%)
  Pallas kernels  27.9 us (29%)
  starting transfers between devices  14.4 us (15%)
  blocking collectives  12.5 us (13%)
  matrix products  2.58 us (3%)
  local copies, waits for them, and re-layouts  2.06 us (2%)
  other arithmetic  1.76 us (2%)
    all_to_all x1, blocking collectives, place(): pieces = lax.all_to_all(pieces, 'blk', 0, 0)  12.5 us
    ppermute x1, waiting for transfers between devices, two_chips(): far = lax.ppermute(send, 'slab', to_chip)  11.8 us
    pallas_call x1, Pallas kernels, two_chips(): pl.pallas_call(functools.partial(factor_rest_kernel, hands), out_shape=ja...  9.79 us
    all_to_all x1, waiting for transfers between devices, place(): pieces = lax.all_to_all(pieces, 'blk', 0, 0)  9.54 us
    pallas_call x1, Pallas kernels, near(): pl.pallas_call(functools.partial(near_kernel, hands), out_shape=(jax.Shap...  8.23 us
    ppermute x1, waiting for transfers between devices, two_chips(): early = lax.ppermute(side_sum, 'slab', to_chip)  7.04 us
    all_to_all x1, starting transfers between devices, place(): pieces = lax.all_to_all(pieces, 'blk', 0, 0)  6.03 us
    pallas_call x2, Pallas kernels, far_product(): pl.pallas_call(far_product_kernel, out_shape=jax.ShapeDtypeStruct((depth,...  5.46 us
  transfers between devices with their start and end apart: 12, of which 5 were waited for; matrix products, arithmetic and copies ran while one was open for 1% of the time, Pallas kernels for 19%

profile of v4, /device:TPU:0, one launch (start us, length us, event | category | flops | bytes accessed | tf_op | source)
XLA Modules:
  0.0 95.6 jit_solution(5339329481941020055)
XLA Ops:
  0.0 0.9 broadcast_select_fusion.3
  0.9 0.8 copy-done
  1.6 1.3 %fusion.7.send_ref = bf16[512,1024]{1,0:T(8,128)(2,1)S(1)} fusion(bf16[1,1024,1024]{2,1,0:T(8,128)(2,1)S(1)} %copy-done, s32[512]{0:T(512)S(1)} %bitcast.25), kind=kOutput, calls=%fused_computation.8 | convolution fusion | flops 1074790400 | bytes 3147776 | tf_op jit(solution)/shard_map/dot_general | solution.py:358
  2.9 1.3 %broadcast_select_fusion = (bf16[512,1024]{1,0:T(8,128)(2,1)S(1)}, bf16[512,1024]{1,0:T(8,128)(2,1)S(1)}) fusion(bf16[512,1024]{1,0:T(8,128)(2,1)S(1)} %fusion.7.send_ref, pred[]{:T(512)S(6)} %eq.48, bf16[1,1024,1024]{2,1,0:T(8,128)(2,1)S(1)} %copy-done, s32[512]{0:T(512)S(1)} %bitcast.24), kind=kOutput, calls=%fused_computation.11 | convolution fusion | flops 1075314688 | bytes 5244929 | tf_op jit(solution)/shard_map/dot_general | solution.py:358
  4.2 0.6 collective-permute-start
  4.8 2.7 %far_product.2 = bf16[1024,512]{1,0:T(8,128)(2,1)S(1)} custom-call(bf16[4096,1024]{1,0:T(8,128)(2,1)} %bitcast.17, bf16[4096,1024]{1,0:T(8,128)(2,1)} %bitcast.20, bf16[512,1024]{1,0:T(8,128)(2,1)S(1)} %get-tuple-element.22.keep_ref), custom_call_target="tpu_custom_call" | custom-call | flops 1073741824 | bytes 4194304 | tf_op jit(solution)/shard_map/far_product/pallas_call | solution.py:336
  7.6 3.0 %collective-permute-start.4 = (bf16[512,1024]{1,0:T(8,128)(2,1)S(1)}, bf16[512,1024]{1,0:T(8,128)(2,1)S(1)}, u32[]{:S(2)}, u32[]{:S(2)}) collective-permute-start(bf16[512,1024]{1,0:T(8,128)(2,1)S(1)} %fusion.7.send_ref), channel_id=1, source_target_pairs={{0,2},{1,3},{2,0},{3,1},{4,6},{5,7},{6,4},{7,5},{8,10},{9,11},{10,... | collective-permute-start | bytes 3145736 | tf_op jit(solution)/shard_map/ppermute | solution.py:382
  10.6 8.2 %near.1 = (f32[520,128]{1,0:T(8,128)S(1)}, f32[520,128]{1,0:T(8,128)S(1)}, f32[520,128]{1,0:T(8,128)S(1)}, f32[520,128]{1,0:T(8,128)S(1)}) custom-call(bf16[4096,1024]{1,0:T(8,128)(2,1)} %bitcast.18, bf16[4096,1024]{1,0:T(8,128)(2,1)} %bitcast.21, bf16[512,1024]{1,0:T(8,128)(2,1)S(1)} %get-tuple-element.22.keep_ref, bf16[512,1024]{1,0:T(8,128)(2,1)S(1)} %fusion.7.send_ref, ...), custom_call_target="tpu_custom_call" | custom-call | flops 4831838208 | bytes 9437184 | tf_op jit(solution)/shard_map/near/pallas_call | solution.py:300
  19.4 2.7 %far_product.3.both_ref = bf16[1024,512]{1,0:T(8,128)(2,1)S(1)} custom-call(bf16[4096,1024]{1,0:T(8,128)(2,1)} %bitcast.19, bf16[4096,1024]{1,0:T(8,128)(2,1)} %bitcast.22, bf16[512,1024]{1,0:T(8,128)(2,1)S(1)} %get-tuple-element.22.keep_ref, bf16[1024,512]{1,0:T(8,128)(2,1)S(1)} %collective-permute-done.5.refs_0_), custom_call_target="tpu_custom_call" | custom-call | flops 1073741824 | bytes 4194304 | tf_op jit(solution)/shard_map/far_product/pallas_call | solution.py:336
  22.2 11.8 %collective-permute-done.4.sel_ref = bf16[512,1024]{1,0:T(8,128)(2,1)S(1)} collective-permute-done((bf16[512,1024]{1,0:T(8,128)(2,1)S(1)}, bf16[512,1024]{1,0:T(8,128)(2,1)S(1)}, u32[]{:S(2)}, u32[]{:S(2)}) %collective-permute-start.4) | collective-permute-done | bytes 1048608 | tf_op jit(solution)/shard_map/ppermute | solution.py:382
  34.0 0.9 far.1
  35.1 1.8 %collective-permute-start.3 = (f32[520,128]{1,0:T(8,128)S(1)}, f32[520,128]{1,0:T(8,128)S(1)}, u32[]{:S(2)}, u32[]{:S(2)}) collective-permute-start(f32[520,128]{1,0:T(8,128)S(1)} %add.27), channel_id=1, source_target_pairs={{0,2},{1,3},{2,0},{3,1},{4,6},{5,7},{6,4},{7,5},{8,10},{9,11},{10,... | collective-permute-start | bytes 798728 | tf_op jit(solution)/shard_map/ppermute | solution.py:389
  36.9 7.0 %collective-permute-done.3 = f32[520,128]{1,0:T(8,128)S(1)} collective-permute-done((f32[520,128]{1,0:T(8,128)S(1)}, f32[520,128]{1,0:T(8,128)S(1)}, u32[]{:S(2)}, u32[]{:S(2)}) %collective-permute-start.3) | collective-permute-done | bytes 266272 | tf_op jit(solution)/shard_map/ppermute | solution.py:389
  44.1 1.8 %collective-permute-start.7 = (f32[256,128]{1,0:T(8,128)S(1)}, f32[256,128]{1,0:T(8,128)S(1)}, u32[]{:S(2)}, u32[]{:S(2)}) collective-permute-start(f32[256,128]{1,0:T(8,128)S(1)} %slice.14), channel_id=1, source_target_pairs={{0,2},{1,3},{2,0},{3,1},{4,6},{5,7},{6,4},{7,5},{8,10},{9,11},{10,... | collective-permute-start | bytes 393224 | tf_op jit(solution)/shard_map/ppermute | solution.py:405
  46.3 4.2 %collective-permute-done.7 = f32[256,128]{1,0:T(8,128)S(1)} collective-permute-done((f32[256,128]{1,0:T(8,128)S(1)}, f32[256,128]{1,0:T(8,128)S(1)}, u32[]{:S(2)}, u32[]{:S(2)}) %collective-permute-start.7) | collective-permute-done | bytes 131104 | tf_op jit(solution)/shard_map/ppermute | solution.py:405
  50.6 1.5 %collective-permute-done.9 = f32[264,128]{1,0:T(8,128)S(1)} collective-permute-done((f32[264,128]{1,0:T(8,128)S(1)}, f32[264,128]{1,0:T(8,128)S(1)}, u32[]{:S(2)}, u32[]{:S(2)}) %collective-permute-start.9) | collective-permute-done | bytes 135200 | tf_op jit(solution)/shard_map/ppermute | solution.py:406
  52.2 0.6 iota_reduce_fusion
  52.8 3.5 %factor_first.1.top_ref = f32[128,512]{1,0:T(8,128)S(1)} custom-call(s32[8]{0:T(128)S(1)} %copy-done.1, f32[256,128]{1,0:T(8,128)S(1)} %slice_multiply_fusion.mine_ref, f32[256,128]{1,0:T(8,128)S(1)} %collective-permute-done.8.theirs_ref), custom_call_target="tpu_custom_call" | custom-call | flops 8388608 | bytes 1048576 | tf_op jit(solution)/shard_map/factor_first/pallas_call | solution.py:409
  56.3 9.8 %factor_rest.1 = f32[128,512]{1,0:T(8,128)} custom-call(s32[8]{0:T(128)S(1)} %copy-done.1, f32[128,512]{1,0:T(8,128)S(1)} %factor_first.1.top_ref, f32[256,128]{1,0:T(8,128)S(1)} %slice_multiply_fusion.mine_ref, f32[256,128]{1,0:T(8,128)S(1)} %collective-permute-done.8.theirs_ref, f32[264,128]{1,0:T(8,128)S(1)} %slice_multiply_fusion.1.mine_rest_ref, ...), custom_call_target="tpu_custom_call" | custom-call | tf_op jit(solution)/shard_map/factor_rest/pallas_call | solution.py:422
  66.1 6.0 %all-to-all-start = ((f32[8,16,512]{2,1,0:T(8,128)}), f32[8,16,512]{2,1,0:T(8,128)S(1)}, u32[]{:S(2)}, u32[]{:S(2)}) async-start(f32[8,16,512]{2,1,0:T(8,128)} %bitcast.5), calls=%async_computation | async-start | bytes 524288 | tf_op jit(solution)/shard_map/all_to_all | solution.py:364
  72.2 9.5 %all-to-all-done = f32[8,16,512]{2,1,0:T(8,128)S(1)} async-done(((f32[8,16,512]{2,1,0:T(8,128)}), f32[8,16,512]{2,1,0:T(8,128)S(1)}, u32[]{:S(2)}, u32[]{:S(2)}) %all-to-all-start) | async-done | bytes 262176 | tf_op jit(solution)/shard_map/all_to_all | solution.py:364
  81.7 0.6 gather_fusion
  82.4 12.5 %all_to_all.10 = f32[8,16,512]{2,1,0:T(8,128)S(1)} all-to-all(f32[8,16,512]{2,1,0:T(8,128)S(1)} %broadcast_select_fusion.1), channel_id=1, replica_groups=mesh['blk'=8,'slab'=4] {'blk'}, dimensions={0} | all-to-all | bytes 524288 | tf_op jit(solution)/shard_map/all_to_all | solution.py:366
  94.9 0.7 copy.8
  (29 shorter events, 1.6 us)
Async XLA Ops:
  0.0 1.6 %copy-start = (bf16[1,1024,1024]{2,1,0:T(8,128)(2,1)S(1)}, bf16[1,1024,1024]{2,1,0:T(8,128)(2,1)}, u32[]{:S(2)}) copy-start(bf16[1,1024,1024]{2,1,0:T(8,128)(2,1)} %param.8) | copy-start | bytes 6291460
  4.2 6.4 %collective-permute-start = (bf16[512,1024]{1,0:T(8,128)(2,1)S(1)}, bf16[512,1024]{1,0:T(8,128)(2,1)S(1)}, u32[]{:S(2)}, u32[]{:S(2)}) collective-permute-start(bf16[512,1024]{1,0:T(8,128)(2,1)S(1)} %get-tuple-element.21), channel_id=1, source_target_pairs={{0,1},{1,0},{2,3},{3,2},{4,5},{5,4},{6,7},{7,6},{8,9},{9,8},{10,11... | collective-permute-start | bytes 3145736 | tf_op jit(solution)/shard_map/ppermute | solution.py:384
  7.5 11.9 %collective-permute-start.5 = (bf16[1024,512]{1,0:T(8,128)(2,1)S(1)}, bf16[1024,512]{1,0:T(8,128)(2,1)S(1)}, u32[]{:S(2)}, u32[]{:S(2)}) collective-permute-start(bf16[1024,512]{1,0:T(8,128)(2,1)S(1)} %far_product.2), channel_id=1, source_target_pairs={{0,1},{1,0},{2,3},{3,2},{4,5},{5,4},{6,7},{7,6},{8,9},{9,8},{10,11... | collective-permute-start | bytes 3145736 | tf_op jit(solution)/shard_map/ppermute | solution.py:386
  7.6 26.4 %collective-permute-start.4 = (bf16[512,1024]{1,0:T(8,128)(2,1)S(1)}, bf16[512,1024]{1,0:T(8,128)(2,1)S(1)}, u32[]{:S(2)}, u32[]{:S(2)}) collective-permute-start(bf16[512,1024]{1,0:T(8,128)(2,1)S(1)} %fusion.7.send_ref), channel_id=1, source_target_pairs={{0,2},{1,3},{2,0},{3,1},{4,6},{5,7},{6,4},{7,5},{8,10},{9,11},{10,... | collective-permute-start | bytes 3145736 | tf_op jit(solution)/shard_map/ppermute | solution.py:382
  18.9 16.2 %collective-permute-start.2 = (f32[520,128]{1,0:T(8,128)S(1)}, f32[520,128]{1,0:T(8,128)S(1)}, u32[]{:S(2)}, u32[]{:S(2)}) collective-permute-start(f32[520,128]{1,0:T(8,128)S(1)} %get-tuple-element.16), channel_id=1, source_target_pairs={{0,1},{1,0},{2,3},{3,2},{4,5},{5,4},{6,7},{7,6},{8,9},{9,8},{10,11... | collective-permute-start | bytes 798728 | tf_op jit(solution)/shard_map/ppermute | solution.py:388
  18.9 18.0 %collective-permute-start.1 = (f32[520,128]{1,0:T(8,128)S(1)}, f32[520,128]{1,0:T(8,128)S(1)}, u32[]{:S(2)}, u32[]{:S(2)}) collective-permute-start(f32[520,128]{1,0:T(8,128)S(1)} %get-tuple-element.14), channel_id=1, source_target_pairs={{0,1},{1,0},{2,3},{3,2},{4,5},{5,4},{6,7},{7,6},{8,9},{9,8},{10,11... | collective-permute-start | bytes 798728 | tf_op jit(solution)/shard_map/ppermute | solution.py:391
  35.0 17.2 %copy-start.2 = (s32[8]{0:T(128)S(1)}, s32[8]{0:T(128)}, u32[]{:S(2)}) copy-start(s32[8]{0:T(128)} %param.11) | copy-start | bytes 100
  35.0 17.8 %copy-start.1 = (s32[8]{0:T(128)S(1)}, s32[8]{0:T(128)}, u32[]{:S(2)}) copy-start(s32[8]{0:T(128)} %orders_ref.3) | copy-start | bytes 100
  35.0 1.9 %collective-permute-start.6 = (f32[520,128]{1,0:T(8,128)S(1)}, f32[520,128]{1,0:T(8,128)S(1)}, u32[]{:S(2)}, u32[]{:S(2)}) collective-permute-start(f32[520,128]{1,0:T(8,128)S(1)} %get-tuple-element.18), channel_id=1, source_target_pairs={{0,1},{1,0},{2,3},{3,2},{4,5},{5,4},{6,7},{7,6},{8,9},{9,8},{10,11... | collective-permute-start | bytes 798728 | tf_op jit(solution)/shard_map/ppermute | solution.py:404
  35.1 8.9 %collective-permute-start.3 = (f32[520,128]{1,0:T(8,128)S(1)}, f32[520,128]{1,0:T(8,128)S(1)}, u32[]{:S(2)}, u32[]{:S(2)}) collective-permute-start(f32[520,128]{1,0:T(8,128)S(1)} %add.27), channel_id=1, source_target_pairs={{0,2},{1,3},{2,0},{3,1},{4,6},{5,7},{6,4},{7,5},{8,10},{9,11},{10,... | collective-permute-start | bytes 798728 | tf_op jit(solution)/shard_map/ppermute | solution.py:389
  44.1 6.4 %collective-permute-start.7 = (f32[256,128]{1,0:T(8,128)S(1)}, f32[256,128]{1,0:T(8,128)S(1)}, u32[]{:S(2)}, u32[]{:S(2)}) collective-permute-start(f32[256,128]{1,0:T(8,128)S(1)} %slice.14), channel_id=1, source_target_pairs={{0,2},{1,3},{2,0},{3,1},{4,6},{5,7},{6,4},{7,5},{8,10},{9,11},{10,... | collective-permute-start | bytes 393224 | tf_op jit(solution)/shard_map/ppermute | solution.py:405
  45.9 6.2 %collective-permute-start.9 = (f32[264,128]{1,0:T(8,128)S(1)}, f32[264,128]{1,0:T(8,128)S(1)}, u32[]{:S(2)}, u32[]{:S(2)}) collective-permute-start(f32[264,128]{1,0:T(8,128)S(1)} %slice.15), channel_id=1, source_target_pairs={{0,2},{1,3},{2,0},{3,1},{4,6},{5,7},{6,4},{7,5},{8,10},{9,11},{10,... | collective-permute-start | bytes 405512 | tf_op jit(solution)/shard_map/ppermute | solution.py:406
  50.5 2.4 %collective-permute-start.8 = (f32[256,128]{1,0:T(8,128)S(1)}, f32[256,128]{1,0:T(8,128)S(1)}, u32[]{:S(2)}, u32[]{:S(2)}) collective-permute-start(f32[256,128]{1,0:T(8,128)S(1)} %slice_multiply_fusion.mine_ref), channel_id=1, source_target_pairs={{0,1},{1,0},{2,3},{3,2},{4,5},{5,4},{6,7},{7,6},{8,9},{9,8},{10,11... | collective-permute-start | bytes 393224 | tf_op jit(solution)/shard_map/ppermute | solution.py:408
  52.1 4.2 %collective-permute-start.10 = (f32[264,128]{1,0:T(8,128)S(1)}, f32[264,128]{1,0:T(8,128)S(1)}, u32[]{:S(2)}, u32[]{:S(2)}) collective-permute-start(f32[264,128]{1,0:T(8,128)S(1)} %slice_multiply_fusion.1.mine_rest_ref), channel_id=1, source_target_pairs={{0,1},{1,0},{2,3},{3,2},{4,5},{5,4},{6,7},{7,6},{8,9},{9,8},{10,11... | collective-permute-start | bytes 405512 | tf_op jit(solution)/shard_map/ppermute | solution.py:421
  66.1 15.6 %all-to-all-start = ((f32[8,16,512]{2,1,0:T(8,128)}), f32[8,16,512]{2,1,0:T(8,128)S(1)}, u32[]{:S(2)}, u32[]{:S(2)}) async-start(f32[8,16,512]{2,1,0:T(8,128)} %bitcast.5), calls=%async_computation | async-start | bytes 524288 | tf_op jit(solution)/shard_map/all_to_all | solution.py:364
